TPU v7x, 32 devices: a whole 2x2x4 slice. The times are simulated.
32 devices in a mesh: img: 4 (over z), band: 8 (over y, x, core).
Axes of the slice: x: 2, y: 2, z: 4, core: 2. Of those that a mesh axis runs over, the one named last changes fastest.
Arguments:
- pixels: bfloat16 [4, 4, 1024, 192], P(None, 'img', 'band'), may hold values from -4 to 4
- valid: int32 [4, 4, 1024, 192], P(None, 'img', 'band'), may hold values from 0 to 1, as said below
- codes: int32 [4, 4, 1024], P(None, 'img', 'band'), may hold values from 0 to 8191
- image_kind: int32 [4, 4], P(None, 'img'), may hold values from 0 to 1
- w_wide: float32 [3584, 2, 512], P(('img', 'band')), may hold values from -0.25 to 0.25
- w_narrow: float32 [2560, 2, 512], P(('img', 'band')), may hold values from -0.25 to 0.25
- w_edge: float32 [512, 448], P(('img', 'band')), may hold values from -0.25 to 0.25
- codebook: float32 [8192, 32], P(('img', 'band')), may hold values from -5 to 5
- norms: float32 [10, 512], replicated, may hold values from 0.25 to 1.75
- bases: float32 [4, 512, 512], replicated, may hold values from -0.25 to 0.25
- basis_edge: float32 [448, 448], replicated, may hold values from -0.25 to 0.25
- m_wide: float32 [3584, 2, 512], P(('img', 'band')), may hold values from -2.3841858e-06 to 2.3841858e-06
- v_wide: float32 [3584, 2, 512], P(('img', 'band')), may hold values from 1.4731672e-13 to 5.8926686e-13
- m_narrow: float32 [2560, 2, 512], P(('img', 'band')), may hold values from -2.3841858e-06 to 2.3841858e-06
- v_narrow: float32 [2560, 2, 512], P(('img', 'band')), may hold values from 1.4731672e-13 to 5.8926686e-13
- m_edge: float32 [512, 448], P(('img', 'band')), may hold values from -2.3841858e-06 to 2.3841858e-06
- v_edge: float32 [512, 448], P(('img', 'band')), may hold values from 1.4731672e-13 to 5.8926686e-13
- m_code: float32 [8192, 32], P(('img', 'band')), may hold values from -5.9604645e-07 to 5.9604645e-07
- v_code: float32 [8192, 32], P(('img', 'band')), may hold values from 9.207295e-15 to 3.682918e-14
- m_norm: float32 [10, 512], replicated, may hold values from -6.67572e-06 to 6.67572e-06
- v_norm: float32 [10, 512], replicated, may hold values from 1.3258505e-12 to 5.303402e-12
Outputs:
- new_wide: float32 [3584, 2, 512], P(('img', 'band'))
- new_m_wide: float32 [3584, 2, 512], P(('img', 'band'))
- new_v_wide: float32 [3584, 2, 512], P(('img', 'band'))
- new_narrow: float32 [2560, 2, 512], P(('img', 'band'))
- new_m_narrow: float32 [2560, 2, 512], P(('img', 'band'))
- new_v_narrow: float32 [2560, 2, 512], P(('img', 'band'))
- new_edge: float32 [512, 448], P(('img', 'band'))
- new_m_edge: float32 [512, 448], P(('img', 'band'))
- new_v_edge: float32 [512, 448], P(('img', 'band'))
- new_codebook: float32 [8192, 32], P(('img', 'band'))
- new_m_code: float32 [8192, 32], P(('img', 'band'))
- new_v_code: float32 [8192, 32], P(('img', 'band'))
- new_norms: float32 [10, 512], replicated
- new_m_norm: float32 [10, 512], replicated
- new_v_norm: float32 [10, 512], replicated
- grad_norm: float32 [], replicated
- loss: float32 [], replicated
Inputs may be any that keep to these rules, and one draw needn't show every extreme that they name: `valid`: 1 where a pixel counts; rows hold more counted pixels towards their end. `image_kind`: 0: the row is one image of 1024 tokens; 1: the row is four images of 256 tokens in order.
All inputs are finite; a program needn't handle non-finite values.
Results may differ from a plain program's by a relative error of at most 0.00075.
The roundings to bfloat16 on the way count: a program that leaves them out, or rounds other values in their place, can miss the bound.
Values may be sent and summed in bfloat16 or wider, within the bound.
A program may use at most 512 MiB of HBM per device.

v0:
```python
import functools

import jax
import jax.numpy as jnp
from jax import lax
from jax.experimental import pallas as pl
from jax.experimental.pallas import tpu as pltpu
from jax.sharding import PartitionSpec as P

HEADS = 8
HDIM = 64
MESH = pl.DeviceIdType.MESH


norm_eps = 1e-05
adam_eps = 1e-08
clip_level = 0.001
beta_first = 0.5
beta_second = 0.6
rate_matrix = 0.02
rate_vector = 0.3
weight_decay = 0.01
commitment = 0.25
masked_score = -1000000000.0
highest = lax.Precision.HIGHEST


def matmul_plain(first_op, second_op):
    return jnp.dot(first_op, second_op, preferred_element_type=jnp.float32)


def matmul_trans(first_op, second_op):
    return lax.dot_general(
        first_op, second_op, (((1,), (1,)), ((), ())), preferred_element_type=jnp.float32
    )


def matmul_outer(first_op, second_op):
    return lax.dot_general(
        first_op, second_op, (((0,), (0,)), ((), ())), preferred_element_type=jnp.float32
    )


def layer_norm(hidden, scale_gain, offset):
    centred = hidden - jnp.mean(hidden, axis=-1, keepdims=True)
    spread = jnp.mean(centred * centred, axis=-1, keepdims=True)
    return centred * lax.rsqrt(spread + norm_eps) * scale_gain + offset


def gelu_tanh(inputs):
    return (
        0.5
        * inputs
        * (1.0 + jnp.tanh(0.7978845608028654 * (inputs + 0.044715 * inputs * inputs * inputs)))
    )


def split_heads(matrix):
    return matrix.reshape(matrix.shape[0], HEADS, HDIM)


def head_scores(q_heads, k_heads, allowed):
    scores = jnp.einsum(
        "qhd,khd->hqk", q_heads, k_heads, preferred_element_type=jnp.float32
    ) * HDIM ** (-0.5)
    return jnp.where(allowed[None], scores, masked_score)


def attend(queries, key_rows, value_rows, allowed):
    scores = head_scores(split_heads(queries), split_heads(key_rows), allowed)
    score_peak = jnp.max(scores, axis=-1, keepdims=True)
    expo = jnp.exp(scores - score_peak)
    total = jnp.sum(expo, axis=-1, keepdims=True)
    softmaxed = (expo / total).astype(jnp.bfloat16)
    attended = jnp.einsum(
        "hqk,khd->qhd", softmaxed, split_heads(value_rows), preferred_element_type=jnp.float32
    )
    return (
        attended.reshape(queries.shape[0], -1).astype(jnp.bfloat16),
        score_peak + jnp.log(total),
    )


def attend_back(queries, key_rows, value_rows, allowed, log_total, grad_out):
    q_heads = split_heads(queries)
    k_heads = split_heads(key_rows)
    v_heads = split_heads(value_rows)
    g_heads = split_heads(grad_out)
    softmaxed = jnp.exp(head_scores(q_heads, k_heads, allowed) - log_total)
    grad_soft = jnp.einsum("qhd,khd->hqk", g_heads, v_heads, preferred_element_type=jnp.float32)
    row_dot = jnp.sum(softmaxed * grad_soft, axis=-1, keepdims=True)
    grad_scores = (softmaxed * (grad_soft - row_dot)).astype(jnp.bfloat16)
    scale = HDIM ** (-0.5)
    grad_q = (
        jnp.einsum("hqk,khd->qhd", grad_scores, k_heads, preferred_element_type=jnp.float32) * scale
    )
    grad_k = (
        jnp.einsum("hqk,qhd->khd", grad_scores, q_heads, preferred_element_type=jnp.float32) * scale
    )
    grad_v = jnp.einsum(
        "hqk,qhd->khd", softmaxed.astype(jnp.bfloat16), g_heads, preferred_element_type=jnp.float32
    )
    return (
        grad_q.reshape(queries.shape[0], -1),
        grad_k.reshape(key_rows.shape[0], -1),
        grad_v.reshape(key_rows.shape[0], -1),
    )


def block_forward(hidden_all, part, wide_rows, narrow_rows, gain_rows, allowed):
    model_width = hidden_all.shape[1]
    own_rows = allowed.shape[0]
    normed_all = layer_norm(hidden_all, gain_rows[0], gain_rows[1]).astype(jnp.bfloat16)
    hidden = lax.dynamic_slice_in_dim(hidden_all, part * own_rows, own_rows, 0)
    normed = lax.dynamic_slice_in_dim(normed_all, part * own_rows, own_rows, 0)
    queries = matmul_trans(normed, wide_rows[:model_width]).astype(jnp.bfloat16)
    key_rows = matmul_trans(normed_all, wide_rows[model_width : 2 * model_width]).astype(jnp.bfloat16)
    value_rows = matmul_trans(normed_all, wide_rows[2 * model_width : 3 * model_width]).astype(jnp.bfloat16)
    attended, log_total = attend(queries, key_rows, value_rows, allowed)
    middle = hidden + matmul_plain(attended, narrow_rows[:model_width])
    second = layer_norm(middle, gain_rows[2], gain_rows[3]).astype(jnp.bfloat16)
    upper_in = matmul_trans(second, wide_rows[3 * model_width :])
    active = gelu_tanh(upper_in).astype(jnp.bfloat16)
    result = middle + matmul_plain(active, narrow_rows[model_width:])
    return (
        result,
        (hidden, normed, queries, key_rows, value_rows, attended, log_total, middle, second, upper_in, active),
    )


def block_backward(grad_out, wide_rows, narrow_rows, gain_rows, allowed, saved, groups):
    (hidden, normed, queries, key_rows, value_rows, attended, log_total, middle, second, upper_in, active) = saved
    model_width = hidden.shape[1]
    grad_y = grad_out.astype(jnp.bfloat16)
    grad_down = matmul_outer(active, grad_y)
    grad_active = matmul_trans(grad_y, narrow_rows[model_width:])
    grad_upper = jax.vjp(gelu_tanh, upper_in)[1](grad_active)[0].astype(jnp.bfloat16)
    grad_up = matmul_outer(grad_upper, second)
    _, second_back = jax.vjp(layer_norm, middle, gain_rows[2], gain_rows[3])
    grad_mid, gain_two, offset_two = second_back(
        matmul_plain(grad_upper, wide_rows[3 * model_width :])
    )
    grad_mid = grad_mid + grad_out
    grad_attn = grad_mid.astype(jnp.bfloat16)
    grad_outproj = matmul_outer(attended, grad_attn)
    grad_att = matmul_trans(grad_attn, narrow_rows[:model_width]).astype(jnp.bfloat16)
    grad_q, grad_keys, grad_values = attend_back(
        queries, key_rows, value_rows, allowed, log_total, grad_att
    )
    grad_k = lax.psum_scatter(grad_keys, "band", scatter_dimension=0, tiled=True, axis_index_groups=groups)
    grad_v = lax.psum_scatter(grad_values, "band", scatter_dimension=0, tiled=True, axis_index_groups=groups)
    grad_mixed = jnp.concatenate([grad_q, grad_k, grad_v], axis=1).astype(jnp.bfloat16)
    grad_qkv = matmul_outer(grad_mixed, normed)
    _, first_back = jax.vjp(layer_norm, hidden, gain_rows[0], gain_rows[1])
    grad_in, gain_one, offset_one = first_back(
        matmul_plain(grad_mixed, wide_rows[: 3 * model_width])
    )
    gain_grads = jnp.stack([gain_one, offset_one, gain_two, offset_two], axis=0)
    return (
        grad_in + grad_mid,
        jnp.concatenate([grad_qkv, grad_up], axis=0),
        jnp.concatenate([grad_outproj, grad_down], axis=0),
        gain_grads,
    )


def pick_codes(code_rows, book_wide, code_width):
    fold = book_wide.shape[1] // code_width
    one_hot = (
        (code_rows // fold)[:, None] == jnp.arange(book_wide.shape[0], dtype=jnp.int32)[None, :]
    ).astype(jnp.bfloat16)
    lane_fold = jnp.arange(book_wide.shape[1], dtype=jnp.int32)[None, :] // code_width
    lane_mask = (code_rows % fold)[:, None] == lane_fold
    spread = jnp.where(lane_mask, matmul_plain(one_hot, book_wide), 0.0)
    chosen = sum(spread[:, k * code_width : (k + 1) * code_width] for k in range(fold))
    return chosen, one_hot, lane_mask


def row_step(gathered, norms, pixel_all, valid_rows, code_all, part, allowed, count, latent_total, groups):
    wide_all, narrow_all, edge_all, book_wide = gathered
    patch_size = pixel_all.shape[1]
    code_width = edge_all.shape[1] // 2 - patch_size
    own_rows = allowed.shape[0]
    edge_in = edge_all[:, :patch_size]
    edge_pix = edge_all[:, patch_size : 2 * patch_size]
    edge_qin = edge_all[:, 2 * patch_size : 2 * patch_size + code_width]
    edge_qout = edge_all[:, 2 * patch_size + code_width :]
    pixel_rows = lax.dynamic_slice_in_dim(pixel_all, part * own_rows, own_rows, 0)
    chosen_all, one_hot_all, lane_mask_all = pick_codes(code_all, book_wide, code_width)
    chosen_low_all = chosen_all.astype(jnp.bfloat16)
    chosen = lax.dynamic_slice_in_dim(chosen_all, part * own_rows, own_rows, 0)
    one_hot = lax.dynamic_slice_in_dim(one_hot_all, part * own_rows, own_rows, 0)
    lane_mask = lax.dynamic_slice_in_dim(lane_mask_all, part * own_rows, own_rows, 0)
    chosen_low = chosen.astype(jnp.bfloat16)
    begin = matmul_trans(chosen_low_all, edge_qout)
    decoded, dec_saved = block_forward(begin, part, wide_all[1], narrow_all[1], norms[4:8], allowed)
    final = layer_norm(decoded, norms[8], norms[9]).astype(jnp.bfloat16)
    predict = matmul_plain(final, edge_pix)
    error = predict - pixel_rows.astype(jnp.float32)
    pixel_mask = valid_rows.astype(jnp.float32)
    loss_pix = jnp.sum(pixel_mask * (error * error + jnp.abs(error))) / count
    grad_pred = (pixel_mask * (2.0 * error + jnp.sign(error)) / count).astype(jnp.bfloat16)
    grad_pixw = matmul_outer(final, grad_pred)
    _, final_back = jax.vjp(layer_norm, decoded, norms[8], norms[9])
    grad_dec, gain_last, offset_last = final_back(matmul_trans(grad_pred, edge_pix))
    grad_begin, dec_wide, dec_narrow, dec_gains = block_backward(
        grad_dec, wide_all[1], narrow_all[1], norms[4:8], allowed, dec_saved, groups
    )
    grad_begin_low = grad_begin.astype(jnp.bfloat16)
    grad_qout = matmul_outer(grad_begin_low, chosen_low)
    start = matmul_trans(pixel_all, edge_in)
    encoded, enc_saved = block_forward(start, part, wide_all[0], narrow_all[0], norms[0:4], allowed)
    encoded_low = encoded.astype(jnp.bfloat16)
    latent = matmul_plain(encoded_low, edge_qin)
    gap = chosen - latent
    loss_part = loss_pix + (1.0 + commitment) * jnp.sum(gap * gap) / latent_total
    grad_latent = (
        matmul_plain(grad_begin_low, edge_qout) - 2.0 * commitment * gap / latent_total
    ).astype(jnp.bfloat16)
    fold = lane_mask.shape[1] // code_width
    gap_wide = jnp.where(lane_mask, jnp.tile(2.0 * gap / latent_total, (1, fold)), 0.0)
    gap_high = gap_wide.astype(jnp.bfloat16)
    gap_rest = gap_wide - gap_high.astype(jnp.float32)
    gap_middle = gap_rest.astype(jnp.bfloat16)
    gap_low = (gap_rest - gap_middle.astype(jnp.float32)).astype(jnp.bfloat16)
    grad_book = (
        matmul_outer(one_hot, gap_high) + matmul_outer(one_hot, gap_middle)
    ) + matmul_outer(one_hot, gap_low)
    grad_qin = matmul_outer(encoded_low, grad_latent)
    grad_start, enc_wide, enc_narrow, enc_gains = block_backward(
        matmul_trans(grad_latent, edge_qin), wide_all[0], narrow_all[0], norms[0:4], allowed, enc_saved, groups
    )
    grad_inw = matmul_outer(grad_start.astype(jnp.bfloat16), pixel_rows)
    grads = (
        enc_wide, dec_wide, enc_narrow, dec_narrow,
        jnp.concatenate([grad_inw, grad_pixw, grad_qin, grad_qout], axis=1),
        grad_book,
    )
    norm_grad = jnp.concatenate([enc_gains, dec_gains, gain_last[None], offset_last[None]], axis=0)
    return (grads, norm_grad, loss_part)


def place():
    img_at = lax.axis_index("img")
    band_at = lax.axis_index("band")
    return img_at, band_at, band_at // 4, (band_at // 2) % 2, band_at % 2


def neighbours():
    img_at, band_at, y_at, x_at, c_at = place()
    return (
        (img_at, band_at + 1 - 2 * c_at),
        (img_at, band_at + 2 - 4 * x_at),
        (img_at, band_at + 4 - 8 * y_at),
    )


def peers():
    img_at, band_at = place()[:2]
    found = [((img_at + step) % 4, band_at) for step in range(1, 4)]
    return found + [(img_at, (band_at + step) % 8) for step in range(1, 8)]


def meet(others):
    barrier = pltpu.get_barrier_semaphore()
    for other in others:
        pl.semaphore_signal(barrier, inc=1, device_id=other, device_id_type=MESH)
    pl.semaphore_wait(barrier, len(others))


def far_copy(src, dst, send, recv, target):
    return pltpu.make_async_remote_copy(
        src_ref=src, dst_ref=dst, send_sem=send, recv_sem=recv, device_id=target, device_id_type=MESH
    )


class Everywhere:
    def __init__(self, name, agenda, own_ref, img_buf, band_buf, send, recv, result_ref):
        self.name, self.agenda, self.done = name, agenda, False
        self.own, self.img_buf, self.band_buf, self.result = own_ref, img_buf, band_buf, result_ref
        self.send, self.recv = send, recv

    def begin(self):
        img_at, band_at = place()[:2]
        self.img_buf[img_at] = self.own[...]
        copies = [
            far_copy(
                self.own, self.img_buf.at[img_at], self.send.at[step], self.recv.at[step], ((img_at + step) % 4, band_at)
            )
            for step in range(1, 4)
        ]
        self.agenda.launch((self.name, 0), copies, [], self.middle)
        self.agenda.spend(0.5)

    def middle(self):
        img_at, band_at = place()[:2]
        buf = self.img_buf
        self.result[...] = (buf[0] + buf[1]) + (buf[2] + buf[3])
        self.band_buf[band_at] = self.result[...]
        copies = [
            far_copy(
                self.result, self.band_buf.at[band_at], self.send.at[3 + step], self.recv.at[3 + step],
                (img_at, (band_at + step) % 8),
            )
            for step in range(1, 8)
        ]
        self.agenda.launch((self.name, 1), copies, [], self.end)
        self.agenda.spend(1.0)

    def end(self):
        total = self.band_buf[0]
        for k in range(1, 8):
            total = total + self.band_buf[k]
        self.result[...] = total
        self.done = True

    def until(self):
        self.agenda.until(lambda: self.done)


LINK, CORE, LAG = 90e3, 500e3, 0.8
SPREAD = {"f01": 3, "f12": 4, "f23": 3, "b10": 3, "b21": 4, "b32": 3}
TOWARDS = (
    {"b10": 3, "b21": 2, "b32": 1},
    {"f01": 1, "b21": 2, "b32": 1},
    {"f01": 1, "f12": 2, "b32": 1},
    {"f01": 1, "f12": 2, "f23": 3},
)


def z_loads(table, size):
    return [(link, count * size) for link, count in table.items()]


class Agenda:
    def __init__(self):
        self.now, self.free, self.flying = 0.0, {}, {}

    def launch(self, key, copies, loads, then):
        done = self.now
        for link, size in loads:
            begin = max(self.now, self.free.get(link, 0.0))
            self.free[link] = begin + size / (CORE if link == "c" else LINK) + 0.4
            done = max(done, self.free[link])
        for copy in copies:
            copy.start()
        self.flying[key] = (done + LAG, copies, then)

    def land(self, key):
        done, copies, then = self.flying.pop(key)
        self.now = max(self.now, done) + 0.5
        for copy in copies:
            copy.wait()
        then()

    def spend(self, time):
        self.now += time

    def tick(self):
        while self.flying:
            key = min(self.flying, key=lambda name: self.flying[name][0])
            if self.flying[key][0] > self.now:
                return
            self.land(key)

    def until(self, test):
        while not test():
            self.land(min(self.flying, key=lambda name: self.flying[name][0]))


class Gather:
    def __init__(self, name, agenda, pieces, near, z_send, z_recv, p_send, p_recv):
        self.name, self.agenda, self.pieces = name, agenda, pieces
        self.near, self.z_send, self.z_recv, self.p_send, self.p_recv = near, z_send, z_recv, p_send, p_recv
        self.done = set()

    def launch(self, p, k):
        img_at, band_at, y_at, x_at, c_at = place()
        over_c, over_x, over_y = neighbours()
        shard, whole, first, count, z_last = self.pieces[p]
        rows = pl.ds(first, count)
        width = shard.shape[1]
        size = count * max(width, 128) * 2
        lanes = width // 256 * 128
        found, loads = [], []
        here, own = whole.at[img_at, y_at, x_at, c_at, rows], shard.at[rows]
        if z_last and k < 2:
            for half in range(2):
                span = pl.ds(lanes, width - lanes) if half else pl.ds(0, lanes)
                along_y = (k == 0) == (half == 0)
                if k == 0:
                    src, dst = shard.at[rows, span], whole.at[img_at, y_at, x_at, c_at, rows, span]
                elif half == 0:
                    src = dst = whole.at[img_at, :, x_at, c_at, rows, span]
                else:
                    src = dst = whole.at[img_at, y_at, :, c_at, rows, span]
                slot = 2 * k + half
                target = over_y if along_y else over_x
                found.append(far_copy(src, dst, self.p_send.at[p, slot], self.p_recv.at[p, slot], target))
                loads.append(("y" if along_y else "x", (1 + k) * size))
            if k == 0:
                found.append(pltpu.make_async_copy(own, here, self.near.at[p]))
        elif z_last and k == 2:
            part = whole.at[img_at, :, :, c_at, rows]
            found = [
                far_copy(part, part, self.z_send.at[p, step], self.z_recv.at[p, step], ((img_at + step) % 4, band_at))
                for step in range(1, 4)
            ]
            loads = z_loads(SPREAD, 8 * size)
        elif k == 0:
            found = [
                far_copy(own, here, self.z_send.at[p, step], self.z_recv.at[p, step], ((img_at + step) % 4, band_at))
                for step in range(1, 4)
            ]
            found.append(pltpu.make_async_copy(own, here, self.near.at[p]))
            loads = z_loads(SPREAD, 2 * size)
        elif k == 3:
            part = whole.at[:, :, :, c_at, rows]
            found = [far_copy(part, part, self.p_send.at[p, 4], self.p_recv.at[p, 4], over_c)]
            loads = [("c", 16 * size)]
        else:
            for half in range(2):
                span = pl.ds(lanes, width - lanes) if half else pl.ds(0, lanes)
                if lanes == 0 and half == 0:
                    continue
                if k == 1:
                    part = whole.at[:, y_at, x_at, c_at, rows, span]
                elif half == 0:
                    part = whole.at[:, :, x_at, c_at, rows, span]
                else:
                    part = whole.at[:, y_at, :, c_at, rows, span]
                slot = 2 * (k - 1) + half
                along_y = (k == 1) == (half == 0)
                target = over_y if along_y else over_x
                found.append(far_copy(part, part, self.p_send.at[p, slot], self.p_recv.at[p, slot], target))
                loads.append(("y" if along_y else "x", 4 * k * size))

        def then():
            if k < 3:
                self.launch(p, k + 1)
            else:
                self.done.add(p)

        self.agenda.launch((self.name, p), found, loads, then)

    def begin(self, first, last):
        for p in range(first, last):
            self.launch(p, 0)

    def until(self, *wanted):
        self.agenda.until(lambda: all(p in self.done for p in wanted))


def gather_sems(count):
    dma = pltpu.SemaphoreType.DMA
    return [dma((count,)), dma((count, 4)), dma((count, 4)), dma((count, 5)), dma((count, 5))]


class Reduce:
    def __init__(
        self, agenda, slots, wait_z, full, pair, first_a, first_b, second_a, second_b, ours, last,
        near, p_send, p_recv, z_send, z_recv, free, free_z,
    ):
        self.agenda, self.slots, self.wait_z = agenda, slots, wait_z
        self.full, self.pair, self.ours, self.last = full, pair, ours, last
        self.first, self.second = (first_a, first_b), (second_a, second_b)
        self.near, self.p_send, self.p_recv, self.z_send, self.z_recv = near, p_send, p_recv, z_send, z_recv
        self.free, self.free_z = free, free_z
        self.pieces, self.flying, self.events, self.at_event = [], {}, [], 0
        self.queue, self.opened = [], 0

    def plan(self, pieces):
        self.pieces = pieces
        seen = [0] * 4
        for p, piece in enumerate(pieces):
            piece["slot"] = p % self.slots
            piece["place"] = p % (self.wait_z + 1)
            piece["order"] = seen[piece["z"]]
            seen[piece["z"]] += 1
        for piece in pieces:
            piece["again"] = piece["order"] + 2 < seen[piece["z"]]
        self.opened, self.passed, self.ended = 0, set(), set()
        self.ready = {""}

    def feed(self):
        while self.opened < len(self.pieces):
            p = self.opened
            if self.pieces[p]["needs"] not in self.ready or (p >= self.slots and p - self.slots not in self.passed):
                return
            self.opened += 1
            self.open(p)

    def allow(self, name):
        self.ready.add(name)
        self.feed()

    def rows(self, p):
        return pl.ds(0, self.pieces[p]["rows"])

    def open(self, p):
        piece = self.pieces[p]
        slot, rows = piece["slot"], self.rows(p)
        c_at = place()[4]
        over_c = neighbours()[0]
        if p >= self.slots:
            for k in range(3):
                pl.semaphore_wait(self.free.at[slot, k], 1)
        landing = self.pair.at[slot, :, :, rows]
        send, recv = self.p_send.at[slot, 0], self.p_recv.at[slot, 0]
        if "stage" in piece:
            stage, first, count = piece["stage"], piece["first"], piece["rows"]
            copies = []
            for n in range(4):
                theirs = pl.ds(pl.multiple_of(first + (2 * n + 1 - c_at) * count, 8), count)
                ours = pl.ds(pl.multiple_of(first + (2 * n + c_at) * count, 8), count)
                spot = 0 if n == 0 else 4 + n
                copies.append(
                    far_copy(
                        stage.at[theirs], self.pair.at[slot, n // 2, n % 2, rows], self.p_send.at[slot, spot],
                        self.p_recv.at[slot, spot], over_c,
                    )
                )
                copies.append(
                    pltpu.make_async_copy(
                        stage.at[ours], self.full.at[slot, n // 2, n % 2, c_at, rows], self.near.at[slot, n]
                    )
                )
        else:
            piece["emit"](self.full, slot)
            copies = [far_copy(self.full.at[slot, :, :, 1 - c_at, rows], landing, send, recv, over_c)]
        size = piece["rows"] * self.full.shape[5] * 4
        self.agenda.launch(("r", p, 0), copies, [("c", 4 * size)], lambda: self.step(0, p))

    def step(self, k, p):
        piece = self.pieces[p]
        slot, rows, z = piece["slot"], self.rows(p), piece["z"]
        size = piece["rows"] * self.full.shape[5] * 4
        img_at, band_at, y_at, x_at, c_at = place()
        over_c, over_x, over_y = neighbours()
        full, half = self.full, self.full.shape[5] // 2
        low, high = pl.ds(0, half), pl.ds(half, half)
        tiles = piece["rows"] // 16

        def tile(n):
            return pl.ds(pl.multiple_of(n % tiles * 16, 16), 16)

        if k == 0:
            def add(n, carry):
                y, x = n // (2 * tiles), n // tiles % 2
                full[slot, y, x, c_at, tile(n)] += self.pair[slot, y, x, tile(n)]
                return carry
            lax.fori_loop(0, 4 * tiles, add, 0)
            parts = (full.at[slot, :, 1 - x_at, c_at, rows, low], full.at[slot, 1 - y_at, :, c_at, rows, high])
            landings = [self.first[n].at[slot, :, rows] for n in range(2)]
            targets = (over_x, over_y)
        elif k == 1:
            def add(n, carry):
                w = n // tiles
                full[slot, w, x_at, c_at, tile(n), low] += self.first[0][slot, w, tile(n)]
                full[slot, y_at, w, c_at, tile(n), high] += self.first[1][slot, w, tile(n)]
                return carry
            lax.fori_loop(0, 2 * tiles, add, 0)
            parts = (full.at[slot, 1 - y_at, x_at, c_at, rows, low], full.at[slot, y_at, 1 - x_at, c_at, rows, high])
            landings = [self.second[n].at[slot, rows] for n in range(2)]
            targets = (over_y, over_x)
        if k < 2:
            copies = [
                far_copy(
                    parts[n], landings[n], self.p_send.at[slot, 1 + 2 * k + n], self.p_recv.at[slot, 1 + 2 * k + n],
                    targets[n],
                )
                for n in range(2)
            ]
            load = 2 * size if k == 0 else size
            self.agenda.launch(("r", p, 1 + k), copies, [("x", load), ("y", load)], lambda: self.step(k + 1, p))
            return
        spot, order = piece["place"], piece["order"] % 2
        mine = self.ours.at[spot, rows]
        owner = (z, band_at)

        def hop(n):
            return far_copy(mine, self.last.at[order, n, rows], self.z_send.at[spot], self.z_recv.at[order, n], owner)

        if k == 2:
            self.agenda.until(lambda: p < self.wait_z + 1 or p - self.wait_z - 1 in self.ended)

            def add(n, carry):
                self.ours[spot, tile(n), low] = full[slot, y_at, x_at, c_at, tile(n), low] + self.second[0][slot, tile(n)]
                self.ours[spot, tile(n), high] = full[slot, y_at, x_at, c_at, tile(n), high] + self.second[1][slot, tile(n)]
                return carry
            lax.fori_loop(0, tiles, add, 0)

            assert p < self.wait_z + 1 or p - self.wait_z - 1 in self.ended

            @pl.when(img_at != z)
            def _():
                if piece["order"] >= 2:
                    pl.semaphore_wait(self.free_z.at[z, order], 1)
                hop((img_at + 3 - z) % 4).start()

            if p + self.slots < len(self.pieces):
                for n, other in enumerate((over_c, over_x, over_y)):
                    pl.semaphore_signal(self.free.at[slot, n], inc=1, device_id=other, device_id_type=MESH)
            self.passed.add(p)
            self.agenda.launch(("r", p, 3), [], z_loads(TOWARDS[z], 2 * size), lambda: self.step(3, p))
            self.feed()
            return

        @pl.when(img_at != z)
        def _():
            hop((img_at + 3 - z) % 4).wait_send()

        @pl.when(img_at == z)
        def _():
            for n in range(3):
                hop(n).wait_recv()

            def add(n, carry):
                piece["out"][tile(n)] = (self.ours[spot, tile(n)] + self.last[order, 0, tile(n)]) + (
                    self.last[order, 1, tile(n)] + self.last[order, 2, tile(n)]
                )
                return carry
            lax.fori_loop(0, tiles, add, 0)
            if piece["again"]:
                for n in range(1, 4):
                    pl.semaphore_signal(
                        self.free_z.at[z, order], inc=1, device_id=((img_at + n) % 4, band_at), device_id_type=MESH
                    )

        self.ended.add(p)


def reduce_scratch(slots, wait_z, rows, width):
    f32 = jnp.float32
    dma = pltpu.SemaphoreType.DMA
    half = width // 2
    return [
        pltpu.VMEM((slots, 2, 2, 2, rows, width), f32),
        pltpu.VMEM((slots, 2, 2, rows, width), f32),
        pltpu.VMEM((slots, 2, rows, half), f32),
        pltpu.VMEM((slots, 2, rows, half), f32),
        pltpu.VMEM((slots, rows, half), f32),
        pltpu.VMEM((slots, rows, half), f32),
        pltpu.VMEM((wait_z + 1, rows, width), f32),
        pltpu.VMEM((2, 3, rows, width), f32),
        dma((slots, 4)),
        dma((slots, 8)), dma((slots, 8)),
        dma((wait_z + 1,)), dma((2, 3)),
        pltpu.SemaphoreType.REGULAR((slots, 3)),
        pltpu.SemaphoreType.REGULAR((4, 2)),
    ]


class ReduceSmall:
    def __init__(self, agenda, grads, shares, own, pair, first_a, first_b, second_a, second_b, last, near, p_send, p_recv, z_send, z_recv):
        self.agenda, self.done = agenda, set()
        self.grads, self.shares, self.own, self.pair = grads, shares, own, pair
        self.first, self.second, self.last = (first_a, first_b), (second_a, second_b), last
        self.near, self.p_send, self.p_recv, self.z_send, self.z_recv = near, p_send, p_recv, z_send, z_recv
        self.flying = {}

    def start(self, p, copies, loads, k):
        size = self.own[p].shape[3] * self.own[p].shape[4] * 4
        self.agenda.launch(("s", p), copies, [(link, n * size) for link, n in loads], lambda: self.step(p, k))

    def open(self, p):
        c_at = place()[4]
        over_c = neighbours()[0]
        self.start(p, [
            far_copy(self.grads[p].at[:, :, :, 1 - c_at], self.pair[p], self.p_send.at[p, 0], self.p_recv.at[p, 0], over_c),
            pltpu.make_async_copy(self.grads[p].at[:, :, :, c_at], self.own[p], self.near.at[p]),
        ], [("c", 16)], 0)

    def step(self, p, k):
        img_at, band_at, y_at, x_at, c_at = place()
        over_c, over_x, over_y = neighbours()
        own = self.own[p]
        rows = own.shape[3]
        span = (pl.ds(0, rows // 2), pl.ds(rows // 2, rows // 2))

        def send(parts, landings, targets, slot):
            copies = [
                far_copy(parts[n], landings[n], self.p_send.at[p, slot + n], self.p_recv.at[p, slot + n], targets[n])
                for n in range(2)
            ]
            self.start(p, copies, [("x", 8 >> k), ("y", 8 >> k)], k + 1)

        if k == 0:
            own[...] += self.pair[p][...]
            send(
                (own.at[:, :, 1 - x_at, span[0]], own.at[:, 1 - y_at, :, span[1]]),
                (self.first[0][p], self.first[1][p]), (over_x, over_y), 1,
            )
        elif k == 1:
            own[:, :, x_at, span[0]] += self.first[0][p][...]
            own[:, y_at, :, span[1]] += self.first[1][p][...]
            send(
                (own.at[:, 1 - y_at, x_at, span[0]], own.at[:, y_at, 1 - x_at, span[1]]),
                (self.second[0][p], self.second[1][p]), (over_y, over_x), 3,
            )
        elif k == 2:
            own[:, y_at, x_at, span[0]] += self.second[0][p][...]
            own[:, y_at, x_at, span[1]] += self.second[1][p][...]
            copies = []
            for n in range(1, 4):
                target = (img_at + n) % 4
                copies.append(
                    far_copy(
                        own.at[target, y_at, x_at], self.last[p].at[n - 1], self.z_send.at[p, n], self.z_recv.at[p, n],
                        (target, band_at),
                    )
                )
            self.start(p, copies, z_loads(SPREAD, 2), 3)
        else:
            last = self.last[p]
            self.done.add(p)
            self.shares[p][...] = (own[img_at, y_at, x_at] + last[0]) + (last[1] + last[2])


def reduce_small_scratch(shapes):
    f32 = jnp.float32
    dma = pltpu.SemaphoreType.DMA
    count = len(shapes)
    groups = [
        [(4, 2, 2, r, w) for r, w in shapes],
        [(4, 2, 2, r, w) for r, w in shapes],
        [(4, 2, r // 2, w) for r, w in shapes],
        [(4, 2, r // 2, w) for r, w in shapes],
        [(4, r // 2, w) for r, w in shapes],
        [(4, r // 2, w) for r, w in shapes],
        [(3, r, w) for r, w in shapes],
    ]
    return [pltpu.VMEM(shape, f32) for group in groups for shape in group] + [
        dma((count,)), dma((count, 5)), dma((count, 5)), dma((count, 4)), dma((count, 4)),
    ]


def dot_nn(a, b):
    return lax.dot_general(a, b, (((1,), (0,)), ((), ())), preferred_element_type=jnp.float32)


def dot_nt(a, b):
    return lax.dot_general(a, b, (((1,), (1,)), ((), ())), preferred_element_type=jnp.float32)


def dot_tn(a, b):
    return lax.dot_general(a, b, (((0,), (0,)), ((), ())), preferred_element_type=jnp.float32)


def norm_parts(h):
    centred = h - jnp.mean(h, axis=-1, keepdims=True)
    rate = lax.rsqrt(jnp.mean(centred * centred, axis=-1, keepdims=True) + norm_eps)
    return centred * rate, rate


def norm_back(grad, h, gain):
    shape, rate = norm_parts(h)
    inner = grad * gain
    back = rate * (
        inner
        - jnp.mean(inner, axis=-1, keepdims=True)
        - shape * jnp.mean(inner * shape, axis=-1, keepdims=True)
    )
    return (
        back,
        jnp.sum(grad * shape, axis=0, keepdims=True),
        jnp.sum(grad, axis=0, keepdims=True),
    )


STEP = 256


def at(k, start=0):
    return pl.ds(pl.multiple_of(start + k * STEP, STEP), STEP)


def lanes_at(k, size, start=0):
    return pl.ds(pl.multiple_of(start + k * size, 128), size)


def loop(first, last, body):
    def step(k, carry):
        body(k)
        return carry

    lax.fori_loop(first, last, step, 0)


class Block:
    def __init__(self, base, source, first_w, small, refs):
        names = (
            "wide", "narrow", "norms", "q_extra", "k_extra", "hidden", "normed", "q_buf", "kv", "mixed_in", "wide_in",
            "middle", "second", "slope", "grad_out", "grad_low", "mid_low", "gatt", "dkv", "dkv_in", "soft", "x_send",
            "x_recv", "x_free",
        )
        for name, ref in zip(names, refs, strict=True):
            setattr(self, name, ref)
        self.base, self.source, self.first_w, self.small = base, source, first_w, small
        self.part = place()[4]
        self.total, self.own = self.kv.shape[0], self.q_buf.shape[0]
        self.width = self.q_buf.shape[1]
        self.offset = pl.multiple_of(self.part * self.own, self.own)
        self.chunks = self.own // STEP
        lane_head = lax.broadcasted_iota(jnp.int32, (1, 128), 1) // HDIM
        self.pick = [jnp.where(lane_head == k, 1.0, 0.0).astype(jnp.bfloat16) for k in range(2)]

    def slope_rows(self, f, k):
        return pl.ds(pl.multiple_of(f * self.own + k * STEP, STEP), STEP)

    def gain(self, k):
        return self.norms[pl.ds(self.base + k, 1), :]

    def add_small(self, row, value):
        self.small[pl.ds(row, 1), :] += value

    def add_loss(self, value):
        first_lane = lax.broadcasted_iota(jnp.int32, (1, self.width), 1) == 0
        self.add_small(6, jnp.where(first_lane, value, 0.0))

    def enter(self, first, last):
        def body(n):
            k = (n + self.chunks * (1 + self.part)) % (self.total // STEP)
            h = dot_nt(self.source(k), self.first_w())
            self.hidden[at(n % self.chunks)] = h
            shape, _ = norm_parts(h)
            self.normed[at(k)] = (shape * self.gain(0) + self.gain(1)).astype(jnp.bfloat16)

        loop(first, last, body)

    def make_kv(self, first, last):
        def body(k):
            self.kv[at(k)] = dot_nt(self.normed[at(k)], self.wide[self.width : 3 * self.width]).astype(jnp.bfloat16)

        loop(first, last, body)

    def make_q(self):
        def body(k):
            q = dot_nt(self.normed[at(k, self.offset)], self.wide[: self.width]).astype(jnp.bfloat16)
            self.q_buf[at(k)] = (q.astype(jnp.float32) * HDIM**-0.5).astype(jnp.bfloat16)

        loop(0, self.chunks, body)

    def scores(self, p, k, rows, k_cat):
        q_cat = jnp.concatenate([self.q_buf[rows, lanes_at(p, 128)] * self.pick[k], self.q_extra[rows]], axis=1)
        return dot_nt(q_cat, k_cat)

    def key_columns(self, p):
        return jnp.concatenate([self.kv[:, lanes_at(p, 128)], self.k_extra[...]], axis=1)

    def attend(self, first, last):
        head_lane = lax.broadcasted_iota(jnp.int32, (STEP, 128), 1)

        def pair(p):
            k_cat = self.key_columns(p)
            v_pair = self.kv[:, lanes_at(p, 128, self.width)]

            def body(j):
                rows = at(j)
                mixed = None
                for k in range(2):
                    scores = self.scores(p, k, rows, k_cat)
                    peak = jnp.max(scores, axis=-1, keepdims=True)
                    expo = jnp.exp(scores - peak)
                    total = jnp.sum(expo, axis=-1, keepdims=True)
                    prob = expo * (1.0 / total)
                    level = peak + jnp.log(total)
                    self.soft[rows] = jnp.where(head_lane == 2 * p + k, level, self.soft[rows])
                    term = dot_nn(prob.astype(jnp.bfloat16), v_pair * self.pick[k])
                    mixed = term if mixed is None else mixed + term
                self.mixed_in[rows, lanes_at(p, 128)] = mixed.astype(jnp.bfloat16)

            loop(0, self.chunks, body)

        loop(first, last, pair)

    def after_attention(self):
        def body(k):
            rows = at(k)
            mid = self.hidden[at(k)] + dot_nn(self.mixed_in[rows, : self.width], self.narrow[: self.width])
            self.middle[rows] = mid
            shape, _ = norm_parts(mid)
            self.second[rows] = (shape * self.gain(2) + self.gain(3)).astype(jnp.bfloat16)
            self.grad_out[rows] = mid

        loop(0, self.chunks, body)

    def mlp(self, first, last):
        width = self.width

        def body(n):
            f, k = n // self.chunks, n % self.chunks
            rows = at(k)
            u = dot_nt(self.second[rows], self.wide[lanes_at(3 + f, width)])
            squared = u * u
            bend = jnp.tanh(0.7978845608028654 * (u + 0.044715 * squared * u))
            low = (0.5 * u * (1.0 + bend)).astype(jnp.bfloat16)
            self.mixed_in[rows, lanes_at(1 + f, width)] = low
            self.slope[self.slope_rows(f, k)] = 0.5 * (1.0 + bend) + (0.5 * u) * (1.0 - bend * bend) * (
                0.7978845608028654 * (1.0 + (3.0 * 0.044715) * squared)
            )
            self.grad_out[rows] += dot_nn(low, self.narrow[lanes_at(1 + f, width)])

        loop(first * self.chunks, last * self.chunks, body)

    def mlp_back(self, first, last):
        width = self.width

        def body(k):
            rows = at(k)
            gy = self.grad_low[rows]

            def feature_step(f, acc):
                ga = dot_nt(gy, self.narrow[lanes_at(1 + f, width)])
                low = (ga * self.slope[self.slope_rows(f, k)]).astype(jnp.bfloat16)
                self.wide_in[rows, lanes_at(3 + f, width)] = low
                return acc + dot_nn(low, self.wide[lanes_at(3 + f, width)])

            grad_second = lax.fori_loop(0, 4, feature_step, jnp.zeros((STEP, width), jnp.float32))
            back, g_gain, g_offset = norm_back(grad_second, self.middle[rows], self.gain(2))
            self.add_small(2, g_gain)
            self.add_small(3, g_offset)
            grad_mid = back + self.grad_out[rows]
            self.grad_out[rows] = grad_mid
            low = grad_mid.astype(jnp.bfloat16)
            self.mid_low[rows] = low
            self.gatt[rows] = dot_nt(low, self.narrow[:width]).astype(jnp.bfloat16)

        loop(first, last, body)

    def attend_back(self, first, last):
        head_lane = lax.broadcasted_iota(jnp.int32, (self.own, 128), 1)
        lane_head = lax.broadcasted_iota(jnp.int32, (1, 128), 1) // HDIM
        rows, bf16 = slice(None), jnp.bfloat16

        def head(h):
            p = h // 2
            pick = jnp.where(lane_head == h % 2, 1.0, 0.0).astype(bf16)
            k_pair = self.kv[:, lanes_at(p, 128)]
            g_rows = self.gatt[rows, lanes_at(p, 128)] * pick
            q_rows = self.q_buf[rows, lanes_at(p, 128)] * pick
            level = jnp.sum(jnp.where(head_lane == h, self.soft[...], 0.0), axis=-1, keepdims=True)
            scores = dot_nt(
                jnp.concatenate([q_rows, self.q_extra[...]], axis=1), jnp.concatenate([k_pair, self.k_extra[...]], axis=1)
            )
            prob = jnp.exp(scores - level)
            d_prob = dot_nt(g_rows, self.kv[:, lanes_at(p, 128, self.width)])
            dot_row = jnp.sum(prob * d_prob, axis=-1, keepdims=True)
            d_score = (prob * (d_prob - dot_row)).astype(bf16)
            dq = (dot_nn(d_score, k_pair * pick) * HDIM**-0.5).astype(bf16)
            self.dkv[p, 0] += dot_tn(d_score, q_rows)
            self.dkv[p, 1] += dot_tn(prob.astype(bf16), g_rows)
            self.wide_in[rows, lanes_at(p, 128)] = self.wide_in[rows, lanes_at(p, 128)] + dq

        self.dkv[pl.ds(first, 2)] = jnp.zeros((2,) + self.dkv.shape[1:], jnp.float32)
        self.wide_in[:, pl.ds(pl.multiple_of(128 * first, 128), 256)] = jnp.zeros((self.own, 256), bf16)
        loop(2 * first, 2 * last, head)

    def swap(self, p):
        theirs = pl.ds(pl.multiple_of((1 - self.part) * self.own, self.own), self.own)
        return far_copy(
            self.dkv.at[p, :, theirs], self.dkv_in.at[p], self.x_send.at[p], self.x_recv.at[p], neighbours()[0]
        )

    def attend_back_all(self, opening):
        if not opening:
            pl.semaphore_wait(self.x_free, 1)

        def half(n):
            self.attend_back(2 * n, 2 * n + 2)
            for p in range(2):
                self.swap(2 * n + p).start()

        loop(0, 2, half)

    def swap_start(self, first, opening):
        if not opening and first == 0:
            pl.semaphore_wait(self.x_free, 1)
        for p in range(first, first + 2):
            self.swap(p).start()

    def swap_finish(self, closing):
        for p in range(4):
            self.swap(p).wait()

        def body(n):
            p, k = n // self.chunks, n % self.chunks
            for side in range(2):
                total = self.dkv[p, side, at(k, self.offset)] + self.dkv_in[p, side, at(k)]
                self.wide_in[at(k), lanes_at(p, 128, (1 + side) * self.width)] = total.astype(jnp.bfloat16)

        loop(0, 4 * self.chunks, body)
        if not closing:
            pl.semaphore_signal(self.x_free, inc=1, device_id=neighbours()[0], device_id_type=MESH)

    def leave_rows(self, k):
        rows = at(k)
        grad_normed = dot_nn(self.wide_in[rows, : 3 * self.width], self.wide[: 3 * self.width])
        back, g_gain, g_offset = norm_back(grad_normed, self.hidden[at(k)], self.gain(0))
        self.add_small(0, g_gain)
        self.add_small(1, g_offset)
        return (back + self.grad_out[rows]).astype(jnp.bfloat16)

    def wide_product(self, first, count):
        if first < 3 * self.width:
            right = self.normed[pl.ds(self.offset, self.own)]
        else:
            right = self.second[...]
        return dot_tn(self.wide_in[:, first : first + count], right)

    def narrow_product(self, first, count):
        right = self.mid_low if first < self.width else self.grad_low
        return dot_tn(self.mixed_in[:, first : first + count], right[...])


def pieces_of(first, count, border):
    if first < border < first + count:
        return [(first, border - first), (border, first + count - border)]
    return [(first, count)]


def block_scratch(total_rows, own_rows):
    width = 512
    f32, bf16 = jnp.float32, jnp.bfloat16
    shapes = [
        ((own_rows, width), f32),
        ((total_rows, width), bf16),
        ((own_rows, width), bf16),
        ((total_rows, 2 * width), bf16),
        ((own_rows, 5 * width), bf16),
        ((own_rows, 7 * width), bf16),
        ((own_rows, width), f32),
        ((own_rows, width), bf16),
        ((4 * own_rows, width), f32),
        ((own_rows, width), f32),
        ((own_rows, width), bf16),
        ((own_rows, width), bf16),
        ((own_rows, width), bf16),
        ((4, 2, total_rows, 128), f32),
        ((4, 2, own_rows, 128), f32),
        ((own_rows, 128), f32),
    ]
    return [pltpu.VMEM(shape, dtype) for shape, dtype in shapes] + [
        pltpu.SemaphoreType.DMA((4,)), pltpu.SemaphoreType.DMA((4,)), pltpu.SemaphoreType.REGULAR
    ]


DEC_NARROW = ((0, 80, False),)
ENC_WIDE = ((0, 112, False),)
ENC_NARROW = ((0, 80, False),)
DEC_ORDER = (("n", 3), ("n", 1), ("n", 2), ("n", 0), ("w", 3), ("w", 2), ("w", 0), ("w", 1))
ENC_ORDER = (("n", 3), ("n", 1), ("n", 0), ("w", 3), ("w", 2), ("w", 0), ("w", 1), ("n", 2))


def step_kernel(slots, latent_total, *refs):
    shards, slab, code, kinds, norms = refs[:6], refs[6], refs[7], refs[8], refs[9]
    refs = refs[10:]
    share_wide_dec, share_narrow_dec, share_wide, share_narrow, share_edge, share_book, small_all = refs[:7]
    land_wide_dec, land_narrow_dec, land_wide, land_narrow = refs[7:11]
    refs = refs[11:]
    sems_dec, sems_enc, red, red_small, refs = refs[:5], refs[5:10], refs[10:25], refs[25:44], refs[44:]
    (book, edge, slab_all, code_all, tally, tally_all, t_img, t_band, e_near, e_send, e_recv, t_send, t_recv) = refs[:13]
    refs = refs[1:]
    (code_row, spread, cross, g_pixw, g_qout, g_qin, g_inw, g_edge, g_book) = refs[12:21]
    (small_dec, small_enc, small_own, s_img, s_band, s_send, s_recv, load_sem, wide, narrow) = refs[21:31]
    q_extra, k_extra = refs[31:33]
    scratch = refs[33:]
    f32, bf16 = jnp.float32, jnp.bfloat16
    img_at, band_at, y_at, x_at, c_at = place()
    chip_at = band_at // 2
    over_c = neighbours()[0]
    width = wide.shape[1]
    common = (wide, narrow, norms, q_extra, k_extra) + tuple(scratch)

    def edge_columns(first, count):
        return edge[:, :, :, :, :, first : first + count].reshape(width, count)

    def e_in():
        return edge_columns(0, 256)

    def e_pix():
        return edge_columns(256, 256)

    def e_qin():
        return edge_columns(512, 128)

    def e_qout():
        return edge_columns(640, 128)

    def pixel_rows(k, first=0, start=0):
        return slab_all[pl.ds(start + 2 * k, 2), :, first : first + 256].reshape(STEP, 256)

    own_band = 4 * c_at
    dec = Block(4, lambda k: spread[at(k)], e_qout, small_dec, common)
    enc = Block(0, pixel_rows, e_in, small_enc, common)
    agenda = Agenda()
    dec_pieces = [(shards[0], book, 0, 64, False), (shards[1], edge, 0, 16, False)]
    dec_pieces += [(shards[2], land_wide_dec, 96, 16, True)]
    dec_pieces += [(shards[2], land_wide_dec, 0, 48, False), (shards[2], land_wide_dec, 48, 48, False)]
    dec_pieces += [(shards[3], land_narrow_dec, first, count, last) for first, count, last in DEC_NARROW]
    gather = Gather("d", agenda, dec_pieces, *sems_dec)
    enc_pieces = [(shards[4], land_wide, first, count, last) for first, count, last in ENC_WIDE]
    enc_pieces += [(shards[5], land_narrow, first, count, last) for first, count, last in ENC_NARROW]
    gather_enc = Gather("e", agenda, enc_pieces, *sems_enc)
    count_all = Everywhere("n", agenda, tally, t_img, t_band, t_send, t_recv, tally_all)
    spots = lax.broadcasted_iota(jnp.int32, (1, 4), 1)
    kind = jnp.sum(jnp.where(spots == chip_at, kinds[...], 0).astype(f32), axis=1, keepdims=True)
    meet(peers())
    agenda.spend(3.0)
    gather.begin(0, 5)
    exchange = []
    for step in range(1, 4):
        chip = (chip_at + step) % 4
        target = (img_at, 2 * chip + c_at)
        here = band_at
        exchange.append(far_copy(slab.at[chip], slab_all.at[here], e_send.at[0, step], e_recv.at[0, step], target))
        exchange.append(far_copy(code.at[chip], code_all.at[here], e_send.at[1, step], e_recv.at[1, step], target))
    exchange.append(pltpu.make_async_copy(slab.at[chip_at], slab_all.at[band_at], e_near.at[0]))
    exchange.append(pltpu.make_async_copy(code.at[chip_at], code_all.at[band_at], e_near.at[1]))

    def exchange_landed():
        late = []
        for k, dst in enumerate((slab_all, code_all)):
            for chip in range(4):
                part = dst.at[2 * chip + c_at]
                late.append(far_copy(part, part, e_send.at[k, 4 + chip], e_recv.at[k, 4 + chip], over_c))
        agenda.launch("x2", late, [("c", 4e5)], lambda: arrived.append(1))

    arrived = []
    agenda.launch("x1", exchange, [("x", 4e5), ("y", 4e5)], exchange_landed)
    agenda.spend(1.0)
    segment_lane = lax.broadcasted_iota(jnp.int32, (enc.total, 128), 1)
    segment = jnp.where(kind < 0.5, 0, lax.broadcasted_iota(jnp.int32, (enc.total, 128), 0) // (enc.total // 4))
    k_extra[...] = jnp.where(segment_lane == segment, 1.0, 0.0).astype(bf16)
    segment_lane = lax.broadcasted_iota(jnp.int32, (enc.own, 128), 1)
    segment = lax.broadcasted_iota(jnp.int32, (enc.own, 128), 0) + enc.offset
    segment = jnp.where(kind < 0.5, 0, segment // (enc.total // 4))
    q_extra[...] = jnp.where((segment_lane < 4) & (segment_lane != segment), -(2.0**30), 0.0).astype(bf16)
    for ref in (small_dec, small_enc, g_pixw, g_qout, g_qin, g_inw):
        ref[...] = jnp.zeros(ref.shape, f32)
    agenda.spend(2.0)
    agenda.tick()
    agenda.until(lambda: arrived)
    def code_column(k, start=0):
        return jnp.concatenate(
            [jnp.transpose(jnp.broadcast_to(code_all[start + 2 * k + n], (8, 128)))[:, 0:1] for n in range(2)], axis=0
        )

    for n in range(4):
        code_row[:, pl.ds(128 * n, 128)] = code_all[own_band + n]

    def pick_codes(k):
        rows = at(k)
        code_here = code_column(k)
        picks = lax.broadcasted_iota(jnp.int32, (STEP, 512), 1)
        found = jnp.zeros((STEP, 128), f32)
        for z in range(4):
            hot = jnp.where(picks + 512 * z == code_here // 4, 1.0, 0.0).astype(bf16)
            found += dot_nn(hot, book[z].reshape(512, 128))
        lanes = lax.broadcasted_iota(jnp.int32, (STEP, 128), 1) // 32
        spread[rows] = jnp.where(lanes == code_here % 4, found, 0.0).astype(bf16)

    lane = lax.broadcasted_iota(jnp.int32, (4, 128, 256), 2)
    flags = slab_all[pl.ds(own_band, 4), :, 128:384].astype(f32)
    tally[...] = jnp.full(tally.shape, jnp.sum(jnp.where(lane < 64, 0.0, flags)))
    agenda.spend(1.0)
    agenda.tick()
    count_all.begin()
    gather.begin(5, len(dec_pieces))
    gather.until(0)
    agenda.tick()
    loop(0, dec.total // STEP, pick_codes)
    agenda.spend(4.0)
    agenda.tick()
    gather.until(1)
    dec.enter(0, dec.total // STEP)
    agenda.spend(1.9)
    agenda.tick()

    def fetch(landed, ref, sem):
        rows = landed.shape[4]

        def body(n):
            src = landed.at[n // 8, (n // 4) % 2, (n // 2) % 2, n % 2]
            pltpu.make_async_copy(src, ref.at[pl.ds(pl.multiple_of(n * rows, 16), rows)], sem).start()

        loop(0, 32, body)
        return pltpu.make_async_copy(ref, ref, sem)

    reduce = Reduce(agenda, *slots, *red)
    tail = ReduceSmall(
        agenda, (g_edge, g_book), (share_edge, share_book),
        *[red_small[2 * n : 2 * n + 2] for n in range(7)], *red_small[14:],
    )

    def emit_wide(blk, z, full, slot):
        values = [blk.wide_product(*span) for span in pieces_of(896 * z, 896, 3 * width)]
        value = values[0] if len(values) == 1 else jnp.concatenate(values, axis=0)
        full[slot] = value.reshape(2, 2, 2, 112, width)
        agenda.spend(0.6)

    def emit_narrow(blk, z, full, slot):
        values = [blk.narrow_product(*span) for span in pieces_of(640 * z, 640, width)]
        value = values[0] if len(values) == 1 else jnp.concatenate(values, axis=0)
        full[slot, :, :, :, :80] = value.reshape(2, 2, 2, 80, width)
        agenda.spend(0.5)

    pieces = []
    for name, blk, out_wide, out_narrow, order in (
        ("dec", dec, share_wide_dec, share_narrow_dec, DEC_ORDER), ("enc", enc, share_wide, share_narrow, ENC_ORDER)
    ):
        for kind_of, z in order:
            if kind_of == "n":
                needs = name + str(int(z == 0))
                pieces.append(dict(emit=functools.partial(emit_narrow, blk, z), z=z, rows=80, out=out_narrow, needs=needs))
                continue
            piece = dict(z=z, rows=112, out=out_wide, needs=name + str(1 + (z < 2)))
            if name == "dec" and z < 2:
                piece.update(stage=dec.slope, first=896 * z)
            else:
                piece.update(emit=functools.partial(emit_wide, blk, z))
            pieces.append(piece)
    reduce.plan(pieces)

    def spend(time):
        agenda.spend(time)
        agenda.tick()

    def decoder_head(k):
        rows = at(k)
        out = dec.grad_out[rows]
        shape, _ = norm_parts(out)
        final = (shape * norms[pl.ds(8, 1), :] + norms[pl.ds(9, 1), :]).astype(bf16)
        error = dot_nn(final, e_pix()) - pixel_rows(k, 0, own_band).astype(f32)
        lane = lax.broadcasted_iota(jnp.int32, (STEP, 256), 1)
        counted = jnp.where(lane < 192, pltpu.roll(pixel_rows(k, 128, own_band).astype(f32), 192, 1), 0.0)
        number = tally_all[0:1, 0:1]
        dec.add_loss(jnp.sum(counted * (error * error + jnp.abs(error))) / number)
        sign = jnp.where(error > 0.0, 1.0, jnp.where(error < 0.0, -1.0, 0.0))
        grad_pred = (counted * (2.0 * error + sign) / number).astype(bf16)
        g_pixw[...] += dot_tn(final, grad_pred)
        back, g_gain, g_offset = norm_back(dot_nt(grad_pred, e_pix()), out, norms[pl.ds(8, 1), :])
        dec.add_small(4, g_gain)
        dec.add_small(5, g_offset)
        dec.grad_out[rows] = back
        dec.grad_low[rows] = back.astype(bf16)

    def encoder_head(k):
        rows = at(k)
        low = enc.grad_out[rows].astype(bf16)
        lanes = lax.broadcasted_iota(jnp.int32, (STEP, 128), 1) // 32
        mine = lanes == code_column(k, own_band) % 4
        gap = jnp.where(mine, spread[at(k, enc.offset)].astype(f32) - dot_nn(low, e_qin()), 0.0)
        enc.add_loss((1.0 + commitment) * jnp.sum(gap * gap) / latent_total)
        grad_latent = jnp.where(mine, cross[rows] - 2.0 * commitment * gap / latent_total, 0.0).astype(bf16)
        g_qin[...] += dot_tn(low, grad_latent)
        back = dot_nt(grad_latent, e_qin())
        enc.grad_out[rows] = back
        enc.grad_low[rows] = back.astype(bf16)
        gap = 2.0 * gap / latent_total
        high = gap.astype(bf16)
        left = gap - high.astype(f32)
        between = left.astype(bf16)
        enc.gatt[rows, :384] = jnp.concatenate([high, between, (left - between.astype(f32)).astype(bf16)], axis=1)

    def book_rows(k):
        picks = lax.broadcasted_iota(jnp.int32, (STEP, enc.own), 0) + k * STEP
        hot = jnp.where(picks == code_row[...] // 4, 1.0, 0.0).astype(bf16)
        summed = dot_nn(hot, enc.gatt[:, :384])
        value = (summed[:, :128] + summed[:, 128:256]) + summed[:, 256:]
        g_book[k // 2, k % 2] = value.reshape(2, 2, 64, 128)

    def decoder_leave(k):
        low = dec.leave_rows(k)
        cross[at(k)] = dot_nn(low, e_qout())
        g_qout[...] += dot_tn(low, spread[at(k, dec.offset)])

    def encoder_leave(k):
        g_inw[...] += dot_tn(enc.leave_rows(k), pixel_rows(k, 0, own_band))

    gather_enc.begin(0, len(enc_pieces))
    gather.until(2, 3, 4)
    fetch(land_wide_dec, wide, load_sem.at[0]).wait()
    spend(2.0)
    dec.make_kv(0, dec.total // STEP)
    dec.make_q()
    spend(2.9)
    dec.attend(0, 4)
    spend(11.1)
    gather.until(*range(5, len(dec_pieces)))
    fetched = fetch(land_narrow_dec, narrow, load_sem.at[1])
    agenda.spend(1.0)
    fetched.wait()
    dec.after_attention()
    spend(1.1)
    dec.mlp(0, 4)
    spend(5.6)
    count_all.until()
    loop(0, dec.chunks, decoder_head)
    agenda.spend(2.0)
    reduce.allow("dec0")
    agenda.tick()
    dec.mlp_back(0, dec.chunks)
    agenda.spend(6.1)
    reduce.allow("dec1")
    agenda.tick()
    dec.attend_back_all(True)
    spend(15.8)
    gather_enc.until(*range(len(enc_pieces)))
    fetched = fetch(land_narrow, narrow, load_sem.at[1])
    dec.swap_finish(False)
    agenda.spend(2.0)
    for z in range(2):
        values = [dec.wide_product(*span) for span in pieces_of(896 * z, 896, 3 * width)]
        dec.slope[pl.ds(896 * z, 896)] = values[0] if len(values) == 1 else jnp.concatenate(values, axis=0)
    agenda.spend(1.2)
    reduce.allow("dec2")
    agenda.tick()
    loop(0, dec.chunks, decoder_leave)
    fetched_wide = fetch(land_wide, wide, load_sem.at[0])
    spend(2.0)
    emitted = 1 + max(p for p in range(8) if "emit" in pieces[p])
    staged = [p for p in range(8) if "stage" in pieces[p]]
    agenda.until(lambda: reduce.opened >= emitted)
    enc.enter(0, enc.total // STEP)
    spend(1.9)
    fetched_wide.wait()
    enc.make_kv(0, enc.total // STEP)
    enc.make_q()
    fetched.wait()
    spend(2.9)
    enc.attend(0, 4)
    spend(11.1)
    enc.after_attention()
    spend(1.1)
    agenda.until(lambda: reduce.opened > max(staged) and not any(("r", p, 0) in agenda.flying for p in staged))
    enc.mlp(0, 4)
    spend(5.6)
    loop(0, enc.chunks, encoder_head)
    agenda.spend(2.0)
    reduce.allow("enc0")
    agenda.tick()
    loop(0, 8, book_rows)
    tail.open(1)
    spend(2.0)
    enc.mlp_back(0, enc.chunks)
    agenda.spend(6.1)
    reduce.allow("enc1")
    agenda.tick()
    enc.attend_back(0, 2)
    enc.swap_start(0, False)
    spend(7.9)
    enc.attend_back(2, 4)
    enc.swap_start(2, False)
    spend(7.9)
    enc.swap_finish(True)
    agenda.spend(2.0)
    reduce.allow("enc2")
    agenda.tick()
    loop(0, enc.chunks, encoder_leave)
    agenda.spend(2.0)

    def all_groups(value):
        value = value + pltpu.roll(value, 64, 1)
        return value + pltpu.roll(value, 32, 1)

    lane = lax.broadcasted_iota(jnp.int32, (width, 128), 1)
    mixed = jnp.where(lane < 64, g_inw[:, 128:], jnp.where(lane < 96, all_groups(g_qin[...]), all_groups(g_qout[...])))
    for first, value in ((0, g_inw[:, :128]), (128, mixed), (256, g_pixw[:, :128]), (384, g_pixw[:, 128:])):
        g_edge[:, :, :, :, :, pl.ds(first, 128)] = value.reshape(4, 2, 2, 2, 16, 128)
    tail.open(0)
    agenda.until(lambda: len(reduce.ended) == len(pieces) and len(tail.done) == 2)
    shares = (share_wide_dec, share_narrow_dec, share_wide, share_narrow, share_edge, share_book)
    squares = sum(jnp.sum(share[...] * share[...]) for share in shares)
    lane = lax.broadcasted_iota(jnp.int32, (8, width), 1)
    row = lax.broadcasted_iota(jnp.int32, (8, width), 0)
    small_own[0] = small_enc[...]
    small_own[1] = jnp.where((row == 7) & (lane == 0), squares, small_dec[...])
    sum_all = Everywhere("a", agenda, small_own, s_img, s_band, s_send, s_recv, small_all)
    sum_all.begin()
    sum_all.until()


def train_step(shards, slab, code, kinds, norms, latent_total, total_rows, own_rows):
    width = 512
    slots = (4, 4)
    f32, bf16, int32 = jnp.float32, jnp.bfloat16, jnp.int32
    any_space = pl.BlockSpec(memory_space=pl.ANY)
    vmem = pl.BlockSpec(memory_space=pltpu.VMEM)
    shape = jax.ShapeDtypeStruct
    out_shape = [
        shape((112, width), f32), shape((80, width), f32), shape((112, width), f32), shape((80, width), f32),
        shape((16, width), f32), shape((64, 128), f32), shape((2, 8, width), f32),
    ]
    out_shape += [shape((4, 2, 2, 2) + s.shape, s.dtype) for s in shards[2:]]
    dma = pltpu.SemaphoreType.DMA
    mem = pltpu.VMEM
    scratch = gather_sems(5 + len(DEC_NARROW)) + gather_sems(len(ENC_WIDE) + len(ENC_NARROW))
    scratch += reduce_scratch(*slots, 112, width) + reduce_small_scratch([(16, width), (64, 128)])
    scratch += [
        mem((4, 2, 2, 2, 64, 128), bf16), mem((4, 2, 2, 2, 16, 768), bf16),
        mem((8, 128, 384), bf16), mem((8, 1, 128), int32), mem((8, 128), f32), mem((8, 128), f32),
        mem((4, 8, 128), f32), mem((8, 8, 128), f32),
        dma((2,)), dma((2, 8)), dma((2, 8)), dma((11,)), dma((11,)),
        mem((1, own_rows), int32), mem((total_rows, 128), bf16),
        mem((own_rows, 128), f32),
        mem((width, 256), f32), mem((width, 128), f32), mem((width, 128), f32), mem((width, 256), f32),
        mem((4, 2, 2, 2, 16, width), f32), mem((4, 2, 2, 2, 64, 128), f32),
        mem((8, width), f32), mem((8, width), f32), mem((2, 8, width), f32),
        mem((4, 2, 8, width), f32), mem((8, 2, 8, width), f32), dma((11,)), dma((11,)),
        dma((2,)), mem((7 * width, width), bf16), mem((5 * width, width), bf16),
        mem((own_rows, 128), bf16), mem((total_rows, 128), bf16),
    ]
    scratch += block_scratch(total_rows, own_rows)
    return pl.pallas_call(
        functools.partial(step_kernel, slots, latent_total),
        out_shape=out_shape,
        in_specs=[any_space] * 8 + [vmem] * 2,
        out_specs=[vmem] * 7 + [any_space] * 4,
        scratch_shapes=scratch,
        compiler_params=pltpu.CompilerParams(collective_id=0, has_side_effects=True, vmem_limit_bytes=(639 << 20) // 10),
        name="train_step",
    )(*shards, slab, code, kinds, norms)


def moments(gradient, first_old, second_old):
    first_new = beta_first * first_old + (1.0 - beta_first) * gradient
    second_new = beta_second * second_old + (1.0 - beta_second) * gradient * gradient
    return (first_new, second_new, first_new / (jnp.sqrt(second_new) + adam_eps))


def rotated_update(weight, gradient, first_old, second_old, basis_stack):
    turned = jnp.einsum("rld,lde->rle", gradient, basis_stack, precision=highest)
    first_new, second_new, direction = moments(turned, first_old, second_old)
    turned_back = jnp.einsum("rle,lde->rld", direction, basis_stack, precision=highest)
    return (weight - rate_matrix * (turned_back + weight_decay * weight), first_new, second_new)


def plain_update(weight, gradient, first_old, second_old):
    first_new, second_new, direction = moments(gradient, first_old, second_old)
    return (weight - rate_vector * (direction + weight_decay * weight), first_new, second_new)


def update_kernel(*refs):
    count = 20
    ins, refs = refs[:count], refs[count:]
    outs, held, sem = refs[:13], refs[13 : 13 + count], refs[13 + count]
    loads = [pltpu.make_async_copy(src, dst, sem.at[k]) for k, (src, dst) in enumerate(zip(ins, held))]
    for load in loads:
        load.start()
    for load in loads:
        load.wait()
    refs = held + outs
    wide_0, wide_1, narrow_0, narrow_1, edge, small = refs[:6]
    wide, narrow, edge_set, norm_set = refs[6:9], refs[9:12], refs[12:15], refs[15:18]
    bases, basis_edge = refs[18:20]
    new_wide, new_narrow, new_edge, new_norms, scalars = refs[20:23], refs[23:26], refs[26:29], refs[29:32], refs[32]
    norm_grad = jnp.concatenate([small[0, 0:4], small[1, 0:6]], axis=0)
    squares = small[1, 7:8, 0:1] + jnp.sum(norm_grad * norm_grad)
    grad_norm = jnp.sqrt(squares)
    factor = jnp.minimum(1.0, clip_level / grad_norm)
    scalars[0:1] = jnp.broadcast_to(grad_norm, (1, 128))
    scalars[1:2] = jnp.broadcast_to(factor, (1, 128))
    scalars[2:3] = jnp.broadcast_to(small[0, 6:7, 0:1] + small[1, 6:7, 0:1], (1, 128))
    scalars[3:8] = jnp.zeros((5, 128), jnp.float32)

    def halves(value):
        high = value.astype(jnp.bfloat16)
        return high, (value - high.astype(jnp.float32)).astype(jnp.bfloat16)

    def product(left, right, dot):
        (high, low), (right_high, right_low) = halves(left), right
        return dot(high, right_high) + (dot(high, right_low) + dot(low, right_high))

    def turn(weight, gradient, first_old, second_old, basis):
        right = halves(basis)
        turned = product(gradient, right, dot_nn)
        first_new, second_new, direction = moments(turned, first_old, second_old)
        back = product(direction, right, dot_nt)
        return weight - rate_matrix * (back + weight_decay * weight), first_new, second_new

    for k, (olds, news, grads) in enumerate(
        ((wide, new_wide, (wide_0, wide_1)), (narrow, new_narrow, (narrow_0, narrow_1)))
    ):
        for layer in range(2):
            found = turn(
                olds[0][:, layer], factor * grads[layer][...], olds[1][:, layer], olds[2][:, layer], bases[2 * k + layer]
            )
            for ref, value in zip(news, found):
                ref[:, layer] = value
    packed = edge[...]
    grad_edge = jnp.concatenate([packed[:, :192], packed[:, 256:448], packed[:, 192:256]], axis=1)
    found = turn(edge_set[0][...], factor * grad_edge, edge_set[1][...], edge_set[2][...], basis_edge[...])
    for ref, value in zip(new_edge, found):
        ref[...] = value
    found = plain_update(norm_set[0][...], factor * norm_grad, norm_set[1][...], norm_set[2][...])
    for ref, value in zip(new_norms, found):
        ref[...] = value


def update_all(grads, wide, narrow, edge, norms, bases, basis_edge):
    vmem = pl.BlockSpec(memory_space=pltpu.VMEM)
    shape = jax.ShapeDtypeStruct
    sets = wide + narrow + edge + norms
    return pl.pallas_call(
        update_kernel,
        out_shape=[shape(a.shape, a.dtype) for a in sets] + [shape((8, 128), jnp.float32)],
        in_specs=[pl.BlockSpec(memory_space=pl.ANY)] * (len(grads) + len(sets) + 2),
        out_specs=[vmem] * (len(sets) + 1),
        scratch_shapes=[pltpu.VMEM(a.shape, a.dtype) for a in (*grads, *sets, bases, basis_edge)]
        + [pltpu.SemaphoreType.DMA((len(grads) + len(sets) + 2,))],
        compiler_params=pltpu.CompilerParams(vmem_limit_bytes=63 << 20),
        name="update_all",
    )(*grads, *sets, bases, basis_edge)


def body(
    pixels,
    valid,
    codes,
    image_kind,
    w_wide,
    w_narrow,
    w_edge,
    codebook,
    norms,
    bases,
    basis_edge,
    m_wide,
    v_wide,
    m_narrow,
    v_narrow,
    m_edge,
    v_edge,
    m_code,
    v_code,
    m_norm,
    v_norm,
):
    band_count = lax.axis_size("band")
    band_index = lax.axis_index("band")
    row_count = pixels.shape[2]
    length = row_count * band_count
    batch_count = pixels.shape[0]
    group = band_count // batch_count
    row = band_index // group
    part = band_index % group
    own_rows = length // group
    groups = [[k * group + j for j in range(group)] for k in range(batch_count)]
    layer_count = w_wide.shape[1]
    code_width = codebook.shape[1]
    latent_total = batch_count * lax.axis_size("img") * length * code_width
    both = ("img", "band")

    direct = band_count == 8 and lax.axis_size("img") == 4 and batch_count == 4
    shards = [w_wide[:, l].astype(jnp.bfloat16) for l in range(layer_count)]
    shards += [w_narrow[:, l].astype(jnp.bfloat16) for l in range(layer_count)]
    shards += [w_edge.astype(jnp.bfloat16), codebook.astype(jnp.bfloat16).reshape(-1, 4 * code_width)]
    slab = jnp.concatenate([pixels[:, 0], valid[:, 0].astype(jnp.bfloat16)], axis=2)
    patch_size = pixels.shape[3]
    if direct:
        edge = shards[4]
        gap = jnp.zeros((edge.shape[0], 64), edge.dtype)
        qin = edge[:, 2 * patch_size : 2 * patch_size + code_width]
        qout = edge[:, 2 * patch_size + code_width :]
        shards[4] = jnp.concatenate(
            [edge[:, :patch_size], gap, edge[:, patch_size : 2 * patch_size], gap] + [qin] * 4 + [qout] * 4, axis=1
        )
        out = train_step(
            [shards[k] for k in (5, 4, 1, 3, 0, 2)], slab, codes, image_kind.reshape(1, -1), norms, latent_total, length, own_rows
        )
        new = update_all(
            (out[2], out[0], out[3], out[1], out[4], out[6]), (w_wide, m_wide, v_wide), (w_narrow, m_narrow, v_narrow),
            (w_edge, m_edge, v_edge), (norms, m_norm, v_norm), bases, basis_edge,
        )
        scalars = new[12]
        grad_norm, factor, loss_total = scalars[0, 0], scalars[1, 0], scalars[2, 0]
        new_code = plain_update(codebook, factor * out[5].reshape(-1, code_width), m_code, v_code)
        return tuple(new[:9]) + new_code + tuple(new[9:12]) + (grad_norm, loss_total)
    wholes = [lax.all_gather(shard, both, axis=0, tiled=True) for shard in shards]
    count = lax.psum(jnp.sum(valid.astype(jnp.float32)), both)

    def whole_row(local):
        everywhere = lax.all_gather(local, "band", axis=0)
        chosen_row = lax.dynamic_index_in_dim(everywhere, row, axis=1, keepdims=False)
        return chosen_row.reshape((length,) + local.shape[2:])

    slab_all = whole_row(slab)
    code_all = whole_row(codes[:, 0])
    kind = lax.dynamic_index_in_dim(image_kind[:, 0], row, 0, keepdims=False)
    span = jnp.where(kind == 0, length, length // 4)
    positions = jnp.arange(length, dtype=jnp.int32)
    gathered = (wholes[:2], wholes[2:4], wholes[4], wholes[5])
    pixel_all = slab_all[:, :patch_size]
    valid_rows = lax.dynamic_slice_in_dim(slab_all, part * own_rows, own_rows, 0)[:, patch_size:]
    own_positions = part * own_rows + jnp.arange(own_rows, dtype=jnp.int32)
    allowed = (own_positions // span)[:, None] == (positions // span)[None, :]
    local_grads, norm_sum, loss_sum = row_step(
        gathered, norms, pixel_all, valid_rows, code_all, part, allowed, count, latent_total, groups
    )
    shares = [lax.psum_scatter(g, both, scatter_dimension=0, tiled=True) for g in local_grads]
    squares = sum(jnp.sum(share * share) for share in shares)
    norm_total, square_total, loss_total = lax.psum((norm_sum, squares, loss_sum), both)
    grad_sum = (
        jnp.stack([shares[0], shares[1]], axis=1),
        jnp.stack([shares[2], shares[3]], axis=1),
        shares[4],
        shares[5].reshape(-1, code_width),
    )
    grad_norm = jnp.sqrt(square_total + jnp.sum(norm_total * norm_total))
    factor = jnp.minimum(1.0, clip_level / grad_norm)
    grad_wide, grad_narrow, grad_edge, grad_book = grad_sum
    new_wide, new_m_wide, new_v_wide = rotated_update(
        w_wide, factor * grad_wide, m_wide, v_wide, bases[:layer_count]
    )
    new_narrow, new_m_narrow, new_v_narrow = rotated_update(
        w_narrow, factor * grad_narrow, m_narrow, v_narrow, bases[layer_count:]
    )
    new_edge, new_m_edge, new_v_edge = rotated_update(
        w_edge[:, None],
        factor * grad_edge[:, None],
        m_edge[:, None],
        v_edge[:, None],
        basis_edge[None],
    )
    new_book, new_m_code, new_v_code = plain_update(codebook, factor * grad_book, m_code, v_code)
    new_norms, new_m_norm, new_v_norm = plain_update(norms, factor * norm_total, m_norm, v_norm)
    return (
        new_wide,
        new_m_wide,
        new_v_wide,
        new_narrow,
        new_m_narrow,
        new_v_narrow,
        new_edge[:, 0],
        new_m_edge[:, 0],
        new_v_edge[:, 0],
        new_book,
        new_m_code,
        new_v_code,
        new_norms,
        new_m_norm,
        new_v_norm,
        grad_norm,
        loss_total,
    )


def solution(mesh):
    in_specs = (
        P(None, "img", "band", None),
        P(None, "img", "band", None),
        P(None, "img", "band"),
        P(None, "img"),
        P(("img", "band"), None, None),
        P(("img", "band"), None, None),
        P(("img", "band"), None),
        P(("img", "band"), None),
        P(),
        P(),
        P(),
        P(("img", "band"), None, None),
        P(("img", "band"), None, None),
        P(("img", "band"), None, None),
        P(("img", "band"), None, None),
        P(("img", "band"), None),
        P(("img", "band"), None),
        P(("img", "band"), None),
        P(("img", "band"), None),
        P(),
        P(),
    )
    out_specs = (
        P(("img", "band"), None, None),
        P(("img", "band"), None, None),
        P(("img", "band"), None, None),
        P(("img", "band"), None, None),
        P(("img", "band"), None, None),
        P(("img", "band"), None, None),
        P(("img", "band"), None),
        P(("img", "band"), None),
        P(("img", "band"), None),
        P(("img", "band"), None),
        P(("img", "band"), None),
        P(("img", "band"), None),
        P(),
        P(),
        P(),
        P(),
        P(),
    )
    return jax.shard_map(body, mesh=mesh, in_specs=in_specs, out_specs=out_specs, check_vma=False)
```

profile of v0, /device:TPU:0, one launch (start us, length us, event | category | flops | bytes accessed | tf_op | source)
XLA Modules:
  0.0 280.9 jit_solution(15863736727025815960)
XLA Ops:
  0.7 0.8 convert_element_type.25
  1.4 0.1 fusion.2
  1.5 0.1 fusion.3
  1.6 0.7 concatenate.6.refs_1_
  2.3 0.8 convert_element_type.24
  3.0 0.1 copy.58
  3.2 0.7 reshape.48.refs_0_
  3.9 1.0 copy.69
  4.9 0.7 slice_bitcast_fusion.2
  5.6 1.1 copy.68
  6.7 0.7 slice_bitcast_fusion
  7.4 1.1 copy.61
  8.4 1.2 copy.62
  9.7 0.9 pad_maximum_fusion.refs_6_
  10.6 257.9 %train_step.1 = (f32[112,512]{1,0:T(8,128)}, f32[80,512]{1,0:T(8,128)}, f32[112,512]{1,0:T(8,128)}, f32[80,512]{1,0:T(8,128)}, f32[16,512]{1,0:T(8,128)}, /*inde...) custom-call(bf16[64,128]{1,0:T(8,128)(2,1)} %reshape.48.refs_0_, ...), custom_call_target="tpu_custom_call" | custom-call | tf_op jit(solution)/shard_map/train_step/pallas_call | solution.py:1415
  268.5 0.0 copy-start.3
  268.5 0.0 copy-start
  268.5 0.0 copy-start.1
  268.5 0.0 copy-start.2
  268.6 9.5 %update_all.1 = (f32[112,2,512]{2,1,0:T(2,128)}, f32[112,2,512]{2,1,0:T(2,128)}, f32[112,2,512]{2,1,0:T(2,128)}, f32[80,2,512]{2,1,0:T(2,128)}, f32[80,2,512]{2,...) custom-call(f32[112,512]{1,0:T(8,128)} %get-tuple-element.37.refs_0_, ...), custom_call_target="tpu_custom_call" | custom-call | tf_op jit(solution)/shard_map/update_all/pallas_call | solution.py:1505
  278.1 1.3 fusion.4
  279.4 0.0 copy-done.3
  279.4 0.6 broadcast_multiply_fusion
  280.1 0.1 mul.42
  280.2 0.1 copy.63
  280.2 0.0 copy-done
  280.2 0.0 copy-done.1
  280.3 0.0 copy-done.2
  280.3 0.6 multiply_subtract_fusion
  (3 shorter events, 0.0 us)
Async XLA Ops:
  268.5 10.9 %copy-start.3 = (f32[64,128]{1,0:T(8,128)S(1)}, f32[64,128]{1,0:T(8,128)}, u32[]{:S(2)}) copy-start(f32[64,128]{1,0:T(8,128)} %get-tuple-element.53) | copy-start | bytes 98308
  268.5 11.7 %copy-start = (f32[256,32]{0,1:T(8,128)S(1)}, f32[256,32]{0,1:T(8,128)}, u32[]{:S(2)}) copy-start(f32[256,32]{0,1:T(8,128)} %param.28) | copy-start | bytes 98308
  268.5 11.7 %copy-start.1 = (f32[256,32]{0,1:T(8,128)S(1)}, f32[256,32]{0,1:T(8,128)}, u32[]{:S(2)}) copy-start(f32[256,32]{0,1:T(8,128)} %param.39) | copy-start | bytes 98308
  268.5 11.7 %copy-start.2 = (f32[256,32]{0,1:T(8,128)S(1)}, f32[256,32]{0,1:T(8,128)}, u32[]{:S(2)}) copy-start(f32[256,32]{0,1:T(8,128)} %param.38) | copy-start | bytes 98308
where the time goes:
time: 282 us; the launch traced here: 281 us
  Pallas kernels  267 us (95%)
  local copies, waits for them, and re-layouts  8.94 us (3%)
  other arithmetic  3.76 us (1%)
    pallas_call x1, Pallas kernels, train_step(): pl.pallas_call(functools.partial(step_kernel, slots, latent_total), out_s...  258 us
    pallas_call x1, Pallas kernels, update_all(): pl.pallas_call(update_kernel, out_shape=[shape(a.shape, a.dtype) for a in...  9.54 us

commit v1 on v0

--- a/solution.py
+++ b/solution.py
@@ -318,7 +318,7 @@
         self.agenda.until(lambda: self.done)
 
 
-LINK, CORE, LAG = 90e3, 500e3, 0.8
+LINK, CORE, LAG = 100e3, 500e3, 0.6
 SPREAD = {"f01": 3, "f12": 4, "f23": 3, "b10": 3, "b21": 4, "b32": 3}
 TOWARDS = (
     {"b10": 3, "b21": 2, "b32": 1},
@@ -1445,16 +1445,24 @@
     count = 20
     ins, refs = refs[:count], refs[count:]
     outs, held, sem = refs[:13], refs[13 : 13 + count], refs[13 + count]
-    loads = [pltpu.make_async_copy(src, dst, sem.at[k]) for k, (src, dst) in enumerate(zip(ins, held))]
-    for load in loads:
-        load.start()
-    for load in loads:
-        load.wait()
+    loads = {k: [pltpu.make_async_copy(ins[k], held[k], sem.at[k])] for k in range(count) if k != 18}
+    loads[18] = [pltpu.make_async_copy(ins[18].at[k], held[18].at[k], sem.at[18 if k == 0 else 19 + k]) for k in range(4)]
+    order = (5, 15, 16, 17, 4, 12, 13, 14, 19, 0, 1, 6, 7, 8, 18, 2, 3, 9, 10, 11)
+    for k in order:
+        for load in loads[k]:
+            load.start()
+
+    def need(*wanted):
+        for k in wanted:
+            while loads[k]:
+                loads[k].pop(0).wait()
+
     refs = held + outs
     wide_0, wide_1, narrow_0, narrow_1, edge, small = refs[:6]
     wide, narrow, edge_set, norm_set = refs[6:9], refs[9:12], refs[12:15], refs[15:18]
     bases, basis_edge = refs[18:20]
     new_wide, new_narrow, new_edge, new_norms, scalars = refs[20:23], refs[23:26], refs[26:29], refs[29:32], refs[32]
+    need(5, 15, 16, 17)
     norm_grad = jnp.concatenate([small[0, 0:4], small[1, 0:6]], axis=0)
     squares = small[1, 7:8, 0:1] + jnp.sum(norm_grad * norm_grad)
     grad_norm = jnp.sqrt(squares)
@@ -1470,7 +1478,9 @@
 
     def product(left, right, dot):
         (high, low), (right_high, right_low) = halves(left), right
-        return dot(high, right_high) + (dot(high, right_low) + dot(low, right_high))
+        both = dot(jnp.concatenate([high, low], axis=0), right_high)
+        rows = left.shape[0]
+        return both[:rows] + (dot(high, right_low) + both[rows:])
 
     def turn(weight, gradient, first_old, second_old, basis):
         right = halves(basis)
@@ -1479,15 +1489,7 @@
         back = product(direction, right, dot_nt)
         return weight - rate_matrix * (back + weight_decay * weight), first_new, second_new
 
-    for k, (olds, news, grads) in enumerate(
-        ((wide, new_wide, (wide_0, wide_1)), (narrow, new_narrow, (narrow_0, narrow_1)))
-    ):
-        for layer in range(2):
-            found = turn(
-                olds[0][:, layer], factor * grads[layer][...], olds[1][:, layer], olds[2][:, layer], bases[2 * k + layer]
-            )
-            for ref, value in zip(news, found):
-                ref[:, layer] = value
+    need(4, 12, 13, 14, 19)
     packed = edge[...]
     grad_edge = jnp.concatenate([packed[:, :192], packed[:, 256:448], packed[:, 192:256]], axis=1)
     found = turn(edge_set[0][...], factor * grad_edge, edge_set[1][...], edge_set[2][...], basis_edge[...])
@@ -1496,6 +1498,17 @@
     found = plain_update(norm_set[0][...], factor * norm_grad, norm_set[1][...], norm_set[2][...])
     for ref, value in zip(new_norms, found):
         ref[...] = value
+    for k, (olds, news, grads) in enumerate(
+        ((wide, new_wide, (wide_0, wide_1)), (narrow, new_narrow, (narrow_0, narrow_1)))
+    ):
+        for layer in range(2):
+            need(2 * k + layer, 6 + 3 * k, 7 + 3 * k, 8 + 3 * k)
+            loads[18].pop(0).wait()
+            found = turn(
+                olds[0][:, layer], factor * grads[layer][...], olds[1][:, layer], olds[2][:, layer], bases[2 * k + layer]
+            )
+            for ref, value in zip(news, found):
+                ref[:, layer] = value
 
 
 def update_all(grads, wide, narrow, edge, norms, bases, basis_edge):
@@ -1508,7 +1521,7 @@
         in_specs=[pl.BlockSpec(memory_space=pl.ANY)] * (len(grads) + len(sets) + 2),
         out_specs=[vmem] * (len(sets) + 1),
         scratch_shapes=[pltpu.VMEM(a.shape, a.dtype) for a in (*grads, *sets, bases, basis_edge)]
-        + [pltpu.SemaphoreType.DMA((len(grads) + len(sets) + 2,))],
+        + [pltpu.SemaphoreType.DMA((len(grads) + len(sets) + 5,))],
         compiler_params=pltpu.CompilerParams(vmem_limit_bytes=63 << 20),
         name="update_all",
     )(*grads, *sets, bases, basis_edge)

time: 282 us -> 278 us (0.986)
  Pallas kernels: 267 us -> 264 us
where the time goes in v1:
time: 278 us; the launch traced here: 277 us
  Pallas kernels  264 us (95%)
  local copies, waits for them, and re-layouts  8.94 us (3%)
  other arithmetic  3.76 us (1%)
    pallas_call x1, Pallas kernels, train_step(): pl.pallas_call(functools.partial(step_kernel, slots, latent_total), out_s...  257 us
    pallas_call x1, Pallas kernels, update_all(): pl.pallas_call(update_kernel, out_shape=[shape(a.shape, a.dtype) for a in...  7.16 us

profile of v1, /device:TPU:0, one launch (start us, length us, event | category | flops | bytes accessed | tf_op | source)
XLA Modules:
  0.0 277.3 jit_solution(15634634309496583118)
XLA Ops:
  0.7 0.8 convert_element_type.25
  1.4 0.1 fusion.2
  1.5 0.1 fusion.3
  1.6 0.7 concatenate.6.refs_1_
  2.3 0.8 convert_element_type.24
  3.0 0.1 copy.58
  3.2 0.7 reshape.48.refs_0_
  3.9 1.0 copy.69
  4.9 0.7 slice_bitcast_fusion.2
  5.6 1.1 copy.68
  6.7 0.7 slice_bitcast_fusion
  7.4 1.1 copy.61
  8.4 1.2 copy.62
  9.7 0.9 pad_maximum_fusion.refs_6_
  10.6 256.7 %train_step.1 = (f32[112,512]{1,0:T(8,128)}, f32[80,512]{1,0:T(8,128)}, f32[112,512]{1,0:T(8,128)}, f32[80,512]{1,0:T(8,128)}, f32[16,512]{1,0:T(8,128)}, /*inde...) custom-call(bf16[64,128]{1,0:T(8,128)(2,1)} %reshape.48.refs_0_, ...), custom_call_target="tpu_custom_call" | custom-call | tf_op jit(solution)/shard_map/train_step/pallas_call | solution.py:1415
  267.3 0.0 copy-start.3
  267.3 0.0 copy-start
  267.3 0.0 copy-start.1
  267.3 0.0 copy-start.2
  267.3 7.2 %update_all.1 = (f32[112,2,512]{2,1,0:T(2,128)}, f32[112,2,512]{2,1,0:T(2,128)}, f32[112,2,512]{2,1,0:T(2,128)}, f32[80,2,512]{2,1,0:T(2,128)}, f32[80,2,512]{2,...) custom-call(f32[112,512]{1,0:T(8,128)} %get-tuple-element.37.refs_0_, ...), custom_call_target="tpu_custom_call" | custom-call | tf_op jit(solution)/shard_map/update_all/pallas_call | solution.py:1518
  274.5 1.3 fusion.4
  275.8 0.0 copy-done.3
  275.8 0.6 broadcast_multiply_fusion
  276.5 0.1 mul.42
  276.6 0.1 copy.63
  276.6 0.0 copy-done
  276.7 0.0 copy-done.1
  276.7 0.0 copy-done.2
  276.7 0.6 multiply_subtract_fusion
  (3 shorter events, 0.0 us)
Async XLA Ops:
  267.3 8.5 %copy-start.3 = (f32[64,128]{1,0:T(8,128)S(1)}, f32[64,128]{1,0:T(8,128)}, u32[]{:S(2)}) copy-start(f32[64,128]{1,0:T(8,128)} %get-tuple-element.53) | copy-start | bytes 98308
  267.3 9.3 %copy-start = (f32[256,32]{0,1:T(8,128)S(1)}, f32[256,32]{0,1:T(8,128)}, u32[]{:S(2)}) copy-start(f32[256,32]{0,1:T(8,128)} %param.28) | copy-start | bytes 98308
  267.3 9.3 %copy-start.1 = (f32[256,32]{0,1:T(8,128)S(1)}, f32[256,32]{0,1:T(8,128)}, u32[]{:S(2)}) copy-start(f32[256,32]{0,1:T(8,128)} %param.39) | copy-start | bytes 98308
  267.3 9.3 %copy-start.2 = (f32[256,32]{0,1:T(8,128)S(1)}, f32[256,32]{0,1:T(8,128)}, u32[]{:S(2)}) copy-start(f32[256,32]{0,1:T(8,128)} %param.38) | copy-start | bytes 98308

commit v2 on v1

--- a/solution.py
+++ b/solution.py
@@ -1046,7 +1046,7 @@
 
 
 DEC_NARROW = ((0, 80, False),)
-ENC_WIDE = ((0, 112, False),)
+ENC_WIDE = ((96, 16, True), (0, 96, False))
 ENC_NARROW = ((0, 80, False),)
 DEC_ORDER = (("n", 3), ("n", 1), ("n", 2), ("n", 0), ("w", 3), ("w", 2), ("w", 0), ("w", 1))
 ENC_ORDER = (("n", 3), ("n", 1), ("n", 0), ("w", 3), ("w", 2), ("w", 0), ("w", 1), ("n", 2))
@@ -1441,6 +1441,29 @@
     return (weight - rate_vector * (direction + weight_decay * weight), first_new, second_new)
 
 
+def prepare_kernel(wide, narrow, edge, wide_0, wide_1, narrow_0, narrow_1, edge_low):
+    low = jnp.bfloat16
+    wide_0[...], wide_1[...] = wide[:, 0].astype(low), wide[:, 1].astype(low)
+    narrow_0[...], narrow_1[...] = narrow[:, 0].astype(low), narrow[:, 1].astype(low)
+    full = edge[...]
+    gap = jnp.zeros((full.shape[0], 64), full.dtype)
+    parts = [full[:, :192], gap, full[:, 192:384], gap] + [full[:, 384:416]] * 4 + [full[:, 416:448]] * 4
+    edge_low[...] = jnp.concatenate(parts, axis=1).astype(low)
+
+
+def prepare(w_wide, w_narrow, w_edge):
+    vmem = pl.BlockSpec(memory_space=pltpu.VMEM)
+    rows, width = (w_wide.shape[0], w_narrow.shape[0]), w_wide.shape[2]
+    shapes = [(rows[0], width)] * 2 + [(rows[1], width)] * 2 + [(w_edge.shape[0], 768)]
+    return pl.pallas_call(
+        prepare_kernel,
+        out_shape=[jax.ShapeDtypeStruct(shape, jnp.bfloat16) for shape in shapes],
+        in_specs=[vmem] * 3,
+        out_specs=[vmem] * 5,
+        name="prepare",
+    )(w_wide, w_narrow, w_edge)
+
+
 def update_kernel(*refs):
     count = 20
     ins, refs = refs[:count], refs[count:]
@@ -1572,13 +1595,7 @@
     slab = jnp.concatenate([pixels[:, 0], valid[:, 0].astype(jnp.bfloat16)], axis=2)
     patch_size = pixels.shape[3]
     if direct:
-        edge = shards[4]
-        gap = jnp.zeros((edge.shape[0], 64), edge.dtype)
-        qin = edge[:, 2 * patch_size : 2 * patch_size + code_width]
-        qout = edge[:, 2 * patch_size + code_width :]
-        shards[4] = jnp.concatenate(
-            [edge[:, :patch_size], gap, edge[:, patch_size : 2 * patch_size], gap] + [qin] * 4 + [qout] * 4, axis=1
-        )
+        shards = list(prepare(w_wide, w_narrow, w_edge)) + shards[5:]
         out = train_step(
             [shards[k] for k in (5, 4, 1, 3, 0, 2)], slab, codes, image_kind.reshape(1, -1), norms, latent_total, length, own_rows
         )

time: 278 us -> 276 us (level)
  local copies, waits for them, and re-layouts: 8.94 us -> 4.59 us
  Pallas kernels: 264 us -> 267 us
    pallas_call x0 -> x1, Pallas kernels: none -> 3.2 us  [prepare(): pl.pallas_call(prepare_kernel, out_shape=[jax.ShapeDtypeStruct(shape, jnp...]
where the time goes in v2:
time: 276 us; the launch traced here: 275 us
  Pallas kernels  267 us (97%)
  local copies, waits for them, and re-layouts  4.59 us (2%)
  other arithmetic  3 us (1%)
    pallas_call x1, Pallas kernels, train_step(): pl.pallas_call(functools.partial(step_kernel, slots, latent_total), out_s...  257 us
    pallas_call x1, Pallas kernels, update_all(): pl.pallas_call(update_kernel, out_shape=[shape(a.shape, a.dtype) for a in...  7.16 us

profile of v2, /device:TPU:0, one launch (start us, length us, event | category | flops | bytes accessed | tf_op | source)
XLA Modules:
  0.0 275.3 jit_solution(4408923790073324262)
XLA Ops:
  0.7 0.8 convert_element_type.9
  1.4 0.1 copy.54
  1.5 0.7 reshape.44.refs_0_
  2.3 1.1 copy.55
  3.3 3.2 %prepare.1 = (bf16[112,512]{1,0:T(8,128)(2,1)}, bf16[112,512]{1,0:T(8,128)(2,1)}, bf16[80,512]{1,0:T(8,128)(2,1)}, bf16[80,512]{1,0:T(8,128)(2,1)}, bf16[16,768]{1,0:T(8,128)(2,1)}) custom-call(f32[112,2,512]{2,1,0:T(2,128)} %refs_6_.1, f32[80,2,512]{2,1,0:T(2,128)} %refs_9_.3, f32[16,448]{1,0:T(8,128)} %refs_12_.1), custom_call_target="tpu_custom_call" | custom-call | tf_op jit(solution)/shard_map/prepare/pallas_call | solution.py:1458
  6.5 1.2 copy.56
  7.8 0.9 pad_maximum_fusion.refs_6_
  8.7 256.6 %train_step.1 = (f32[112,512]{1,0:T(8,128)}, f32[80,512]{1,0:T(8,128)}, f32[112,512]{1,0:T(8,128)}, f32[80,512]{1,0:T(8,128)}, f32[16,512]{1,0:T(8,128)}, /*inde...) custom-call(bf16[64,128]{1,0:T(8,128)(2,1)} %reshape.44.refs_0_, ...), custom_call_target="tpu_custom_call" | custom-call | tf_op jit(solution)/shard_map/train_step/pallas_call | solution.py:1415
  265.3 0.0 copy-start.3
  265.3 0.0 copy-start
  265.3 0.0 copy-start.1
  265.3 0.0 copy-start.2
  265.4 7.2 %update_all.1 = (f32[112,2,512]{2,1,0:T(2,128)}, f32[112,2,512]{2,1,0:T(2,128)}, f32[112,2,512]{2,1,0:T(2,128)}, f32[80,2,512]{2,1,0:T(2,128)}, f32[80,2,512]{2,...) custom-call(f32[112,512]{1,0:T(8,128)} %get-tuple-element.47.refs_0_, ...), custom_call_target="tpu_custom_call" | custom-call | tf_op jit(solution)/shard_map/update_all/pallas_call | solution.py:1541
  272.5 1.3 fusion.2
  273.9 0.0 copy-done.3
  273.9 0.6 broadcast_multiply_fusion
  274.5 0.1 mul.42
  274.6 0.1 copy.57
  274.7 0.0 copy-done
  274.7 0.0 copy-done.1
  274.7 0.0 copy-done.2
  274.7 0.6 multiply_subtract_fusion
  (1 shorter events, 0.0 us)
Async XLA Ops:
  265.3 8.5 %copy-start.3 = (f32[64,128]{1,0:T(8,128)S(1)}, f32[64,128]{1,0:T(8,128)}, u32[]{:S(2)}) copy-start(f32[64,128]{1,0:T(8,128)} %get-tuple-element.63) | copy-start | bytes 98308
  265.3 9.3 %copy-start = (f32[256,32]{0,1:T(8,128)S(1)}, f32[256,32]{0,1:T(8,128)}, u32[]{:S(2)}) copy-start(f32[256,32]{0,1:T(8,128)} %param.28) | copy-start | bytes 98308
  265.3 9.3 %copy-start.1 = (f32[256,32]{0,1:T(8,128)S(1)}, f32[256,32]{0,1:T(8,128)}, u32[]{:S(2)}) copy-start(f32[256,32]{0,1:T(8,128)} %param.39) | copy-start | bytes 98308
  265.3 9.3 %copy-start.2 = (f32[256,32]{0,1:T(8,128)S(1)}, f32[256,32]{0,1:T(8,128)}, u32[]{:S(2)}) copy-start(f32[256,32]{0,1:T(8,128)} %param.38) | copy-start | bytes 98308

commit v3 on v2

--- a/solution.py
+++ b/solution.py
@@ -1047,7 +1047,7 @@
 
 DEC_NARROW = ((0, 80, False),)
 ENC_WIDE = ((96, 16, True), (0, 96, False))
-ENC_NARROW = ((0, 80, False),)
+ENC_NARROW = ((64, 16, True), (0, 64, False))
 DEC_ORDER = (("n", 3), ("n", 1), ("n", 2), ("n", 0), ("w", 3), ("w", 2), ("w", 0), ("w", 1))
 ENC_ORDER = (("n", 3), ("n", 1), ("n", 0), ("w", 3), ("w", 2), ("w", 0), ("w", 1), ("n", 2))
 

time: 276 us -> 276 us (level)
  no operation moved by 1% of the time
where the time goes in v3:
time: 276 us; the launch traced here: 275 us
  Pallas kernels  267 us (97%)
  local copies, waits for them, and re-layouts  4.59 us (2%)
  other arithmetic  3 us (1%)
    pallas_call x1, Pallas kernels, train_step(): pl.pallas_call(functools.partial(step_kernel, slots, latent_total), out_s...  256 us
    pallas_call x1, Pallas kernels, update_all(): pl.pallas_call(update_kernel, out_shape=[shape(a.shape, a.dtype) for a in...  7.16 us

profile of v3, /device:TPU:0, one launch (start us, length us, event | category | flops | bytes accessed | tf_op | source)
XLA Modules:
  0.0 275.2 jit_solution(9447574993865368368)
XLA Ops:
  0.7 0.8 convert_element_type.9
  1.4 0.1 copy.54
  1.5 0.7 reshape.44.refs_0_
  2.3 1.1 copy.55
  3.3 3.2 %prepare.1 = (bf16[112,512]{1,0:T(8,128)(2,1)}, bf16[112,512]{1,0:T(8,128)(2,1)}, bf16[80,512]{1,0:T(8,128)(2,1)}, bf16[80,512]{1,0:T(8,128)(2,1)}, bf16[16,768]{1,0:T(8,128)(2,1)}) custom-call(f32[112,2,512]{2,1,0:T(2,128)} %refs_6_.1, f32[80,2,512]{2,1,0:T(2,128)} %refs_9_.3, f32[16,448]{1,0:T(8,128)} %refs_12_.1), custom_call_target="tpu_custom_call" | custom-call | tf_op jit(solution)/shard_map/prepare/pallas_call | solution.py:1458
  6.5 1.2 copy.56
  7.8 0.9 pad_maximum_fusion.refs_6_
  8.7 256.4 %train_step.1 = (f32[112,512]{1,0:T(8,128)}, f32[80,512]{1,0:T(8,128)}, f32[112,512]{1,0:T(8,128)}, f32[80,512]{1,0:T(8,128)}, f32[16,512]{1,0:T(8,128)}, /*inde...) custom-call(bf16[64,128]{1,0:T(8,128)(2,1)} %reshape.44.refs_0_, ...), custom_call_target="tpu_custom_call" | custom-call | tf_op jit(solution)/shard_map/train_step/pallas_call | solution.py:1415
  265.1 0.0 copy-start.3
  265.1 0.0 copy-start
  265.1 0.0 copy-start.1
  265.2 0.0 copy-start.2
  265.2 7.2 %update_all.1 = (f32[112,2,512]{2,1,0:T(2,128)}, f32[112,2,512]{2,1,0:T(2,128)}, f32[112,2,512]{2,1,0:T(2,128)}, f32[80,2,512]{2,1,0:T(2,128)}, f32[80,2,512]{2,...) custom-call(f32[112,512]{1,0:T(8,128)} %get-tuple-element.47.refs_0_, ...), custom_call_target="tpu_custom_call" | custom-call | tf_op jit(solution)/shard_map/update_all/pallas_call | solution.py:1541
  272.3 1.3 fusion.2
  273.7 0.0 copy-done.3
  273.7 0.6 broadcast_multiply_fusion
  274.3 0.1 mul.42
  274.4 0.1 copy.57
  274.5 0.0 copy-done
  274.5 0.0 copy-done.1
  274.5 0.0 copy-done.2
  274.5 0.6 multiply_subtract_fusion
  (1 shorter events, 0.0 us)
Async XLA Ops:
  265.1 8.5 %copy-start.3 = (f32[64,128]{1,0:T(8,128)S(1)}, f32[64,128]{1,0:T(8,128)}, u32[]{:S(2)}) copy-start(f32[64,128]{1,0:T(8,128)} %get-tuple-element.63) | copy-start | bytes 98308
  265.1 9.3 %copy-start = (f32[256,32]{0,1:T(8,128)S(1)}, f32[256,32]{0,1:T(8,128)}, u32[]{:S(2)}) copy-start(f32[256,32]{0,1:T(8,128)} %param.28) | copy-start | bytes 98308
  265.1 9.3 %copy-start.1 = (f32[256,32]{0,1:T(8,128)S(1)}, f32[256,32]{0,1:T(8,128)}, u32[]{:S(2)}) copy-start(f32[256,32]{0,1:T(8,128)} %param.39) | copy-start | bytes 98308
  265.2 9.3 %copy-start.2 = (f32[256,32]{0,1:T(8,128)S(1)}, f32[256,32]{0,1:T(8,128)}, u32[]{:S(2)}) copy-start(f32[256,32]{0,1:T(8,128)} %param.38) | copy-start | bytes 98308
